TPU v7x, 512 devices: a whole 4x8x8 slice. The times are simulated.
512 devices in a mesh: depth: 16 (over y, core), cam: 32 (over x, z).
Axes of the slice: x: 4, y: 8, z: 8, core: 2. Of those that a mesh axis runs over, the one named last changes fastest.
Arguments:
- block_rays: int32 [16, 32, 32], P('depth', 'cam'), may hold values from -1 to 127, as said below
- block_offsets: int32 [16, 32, 32], P('depth', 'cam'), may hold values from 0 to 255
- view_order: int32 [32], P('cam'), may hold values from 0 to 1
- ray_frames: float32 [32, 6, 128], P('cam'), may hold values from -6 to 6
- target: float32 [32, 128, 64], P('cam'), may hold values from -3 to 3
- enc_freq: float32 [16, 3, 64], P('depth'), may hold values from -32 to 32
- w_in: bfloat16 [16, 128, 256], P('depth'), may hold values from -0.5 to 0.5
- b_in: float32 [16, 256], P('depth'), may hold values from -3 to 3
- w_mid: bfloat16 [16, 256, 256], P('depth'), may hold values from -0.375 to 0.375
- b_mid: float32 [16, 256], P('depth'), may hold values from -3 to 3
- w_feat: bfloat16 [16, 256, 64], P('depth'), may hold values from -0.375 to 0.375
- w_dens: bfloat16 [16, 256], P('depth'), may hold values from -0.375 to 0.375
Outputs:
- pixels: float32 [32, 128, 64], P('cam', 'depth')
- grad_w_in: float32 [16, 128, 256], P('depth', 'cam')
- grad_b_in: float32 [16, 256], P('depth', 'cam')
- grad_w_mid: float32 [16, 256, 256], P('depth', 'cam')
- grad_b_mid: float32 [16, 256], P('depth', 'cam')
- grad_w_feat: float32 [16, 256, 64], P('depth', 'cam')
- grad_w_dens: float32 [16, 256], P('depth', 'cam')
Inputs may be any that keep to these rules, and one draw needn't show every extreme that they name: `block_rays`: for each region and batch the used slots come first and hold distinct ray numbers of that batch; later slots hold -1. A region's slots over all batches hold at most 256 ray numbers; in every draw some region holds exactly that many, with one batch in it whose 32 slots are all used.
All inputs are finite; a program needn't handle non-finite values.
Results may differ from a plain program's by a relative error of at most 0.011.
Values sent between devices are 32-bit elements; how exact they have to be, the bound alone decides.
No kernel may reach another device: no remote copies, remote signals or barrier semaphores. Data moves between devices by JAX's collectives and lax.ppermute only.
A program may use at most 64 MiB of HBM per device.

v0:
```python
import jax
import jax.numpy as jnp
from jax import lax
from jax.sharding import PartitionSpec as P

BLK = 128


step_length = 1.0 / 64.0


def carried_in(part, axis, combine, identity, reverse):
    count = lax.axis_size(axis)
    place = lax.axis_index(axis)
    ahead = count - 1 - place if reverse else place
    gathered = jax.tree.map(lambda a: lax.all_gather(a, axis), part)
    state = jax.tree.map(lambda a, e: jnp.zeros_like(a) + jnp.asarray(e, a.dtype), part, identity)

    def one(step, state):
        source = count - 1 - step if reverse else step
        return combine(
            state, jax.tree.map(lambda a: lax.dynamic_index_in_dim(a, source, 0, False), gathered)
        )

    return lax.fori_loop(0, ahead, one, state)


def contract_rows(left, right):
    return lax.dot_general(
        left, right, (((0,), (0,)), ((), ())), preferred_element_type=jnp.float32
    )


def contract_cols(left, right):
    return lax.dot_general(
        left, right, (((1,), (1,)), ((), ())), preferred_element_type=jnp.float32
    )


def strict_upper(samples):
    rows_index = lax.broadcasted_iota(jnp.int32, (samples, samples), 0)
    cols_index = lax.broadcasted_iota(jnp.int32, (samples, samples), 1)
    return (rows_index < cols_index).astype(jnp.float32)


def block_forward(geometry, offsets, frequency, w_in, b_in, w_mid, b_mid, w_feat, w_dens):
    block_count = offsets.shape[0]
    samples = BLK
    positions = (
        offsets.astype(jnp.float32)[:, None] + jnp.arange(samples, dtype=jnp.float32)[None, :] + 0.5
    ) * step_length
    phases = jnp.zeros((block_count * samples, frequency.shape[1]), jnp.float32)
    for component in range(3):
        coordinate = (
            geometry[component][:, None] + positions * geometry[component + 3][:, None]
        ).reshape(-1)
        phases = phases + coordinate[:, None] * frequency[component][None, :]
    encoded = jnp.concatenate([jnp.sin(phases), jnp.cos(phases)], axis=1).astype(jnp.bfloat16)
    hidden_one = jax.nn.relu(
        jnp.dot(encoded, w_in, preferred_element_type=jnp.float32) + b_in
    ).astype(jnp.bfloat16)
    hidden_two = jax.nn.relu(
        jnp.dot(hidden_one, w_mid, preferred_element_type=jnp.float32) + b_mid
    ).astype(jnp.bfloat16)
    features = jnp.dot(hidden_two, w_feat, preferred_element_type=jnp.float32)
    dens_pre = jnp.dot(hidden_two, w_dens, preferred_element_type=jnp.float32)
    tau_step = (jax.nn.softplus(dens_pre) * step_length).reshape(block_count, samples)
    before = jnp.dot(tau_step, strict_upper(samples), precision=lax.Precision.HIGHEST)
    weights = jnp.exp(-before) * -jnp.expm1(-tau_step)
    feature_grid = features.reshape(block_count, samples, features.shape[1])
    colour = jnp.einsum("bs,bsf->bf", weights, feature_grid, precision=lax.Precision.HIGHEST)
    through = jnp.exp(-(before[:, -1] + tau_step[:, -1]))
    stored = (
        encoded,
        hidden_one,
        hidden_two,
        feature_grid,
        dens_pre,
        tau_step,
        before,
        weights,
        through,
    )
    return (colour, through, stored)


def block_backward(stored, d_colour, d_through, w_mid, w_feat, w_dens):
    encoded, hidden_one, hidden_two, feature_grid, dens_pre, tau_step, before, weights, through = (
        stored
    )
    projected = jnp.einsum("bsf,bf->bs", feature_grid, d_colour, precision=lax.Precision.HIGHEST)
    behind = jnp.dot(projected * weights, strict_upper(BLK).T, precision=lax.Precision.HIGHEST)
    d_tau = projected * jnp.exp(-(before + tau_step)) - behind - (d_through * through)[:, None]
    d_pre = ((d_tau * step_length).reshape(-1) * jax.nn.sigmoid(dens_pre)).astype(jnp.bfloat16)
    d_feat = (
        (weights[:, :, None] * d_colour[:, None, :])
        .reshape(-1, d_colour.shape[1])
        .astype(jnp.bfloat16)
    )
    grad_feat = contract_rows(hidden_two, d_feat)
    grad_dens = jnp.dot(d_pre, hidden_two, preferred_element_type=jnp.float32)
    d_two = (
        contract_cols(d_feat, w_feat)
        + d_pre.astype(jnp.float32)[:, None] * w_dens.astype(jnp.float32)[None, :]
    )
    d_two = jnp.where(hidden_two > 0, d_two, 0.0).astype(jnp.bfloat16)
    grad_mid = contract_rows(hidden_one, d_two)
    grad_bmid = jnp.sum(d_two.astype(jnp.float32), axis=0)
    d_one = jnp.where(hidden_one > 0, contract_cols(d_two, w_mid), 0.0).astype(jnp.bfloat16)
    grad_in = contract_rows(encoded, d_one)
    grad_bin = jnp.sum(d_one.astype(jnp.float32), axis=0)
    return (grad_in, grad_bin, grad_mid, grad_bmid, grad_feat, grad_dens)


def join_pairs(low_pair, high_pair, descending):
    low_colour, low_through = low_pair
    high_colour, high_through = high_pair
    rising = low_colour + low_through[..., None] * high_colour
    falling = high_colour + high_through[..., None] * low_colour
    return (jnp.where(descending, falling, rising), low_through * high_through)


def shards(
    block_rays,
    block_offsets,
    view_order,
    ray_frames,
    target,
    enc_freq,
    w_in,
    b_in,
    w_mid,
    b_mid,
    w_feat,
    w_dens,
):
    slot_rays = block_rays[0, 0]
    slot_offsets = block_offsets[0, 0]
    own_frames = ray_frames[0]
    targets = target[0]
    weights_here = (enc_freq[0], w_in[0], b_in[0], w_mid[0], b_mid[0], w_feat[0], w_dens[0])
    ray_total = own_frames.shape[1]
    feature_count = targets.shape[1]
    occupied = slot_rays >= 0
    ray_index = jnp.maximum(slot_rays, 0)
    descending = view_order[0] == 1
    geometry = jnp.take(own_frames, ray_index, axis=1)
    colour_blk, through_blk, stored = block_forward(geometry, slot_offsets, *weights_here)
    slot_ray = jnp.where(occupied, slot_rays, ray_total)
    own_colour = (
        jnp.zeros((ray_total, feature_count), jnp.float32).at[slot_ray].add(colour_blk, mode="drop")
    )
    own_through = 1.0 - jnp.zeros((ray_total,), jnp.float32).at[slot_ray].add(
        1.0 - through_blk, mode="drop"
    )
    own_pair = (own_colour, own_through)
    pair_zero = (
        jnp.zeros((ray_total, feature_count), jnp.float32),
        jnp.ones((ray_total,), jnp.float32),
    )

    def rising(earlier, later):
        return join_pairs(earlier, later, descending)

    def falling(earlier, later):
        return join_pairs(later, earlier, descending)

    low_pair = carried_in(own_pair, "depth", rising, pair_zero, False)
    high_pair = carried_in(own_pair, "depth", falling, pair_zero, True)
    near_through = jnp.where(descending, high_pair[1], low_pair[1])
    far_colour = jnp.where(descending, low_pair[0], high_pair[0])
    pixels, unused_through = join_pairs(
        join_pairs(low_pair, own_pair, descending), high_pair, descending
    )
    grad_pixel = pixels - targets
    d_colour_ray = near_through[:, None] * grad_pixel
    d_through_ray = near_through * jnp.sum(grad_pixel * far_colour, axis=1)
    d_colour_blk = jnp.take(d_colour_ray, ray_index, axis=0) * occupied[:, None]
    d_through_blk = jnp.take(d_through_ray, ray_index) * occupied
    gradients = block_backward(
        stored, d_colour_blk, d_through_blk, weights_here[3], weights_here[5], weights_here[6]
    )
    reduced = (
        lax.psum_scatter(gradients[0][None], "cam", scatter_dimension=1, tiled=True),
        lax.psum_scatter(gradients[1][None], "cam", scatter_dimension=1, tiled=True),
        lax.psum_scatter(gradients[2][None], "cam", scatter_dimension=1, tiled=True),
        lax.psum_scatter(gradients[3][None], "cam", scatter_dimension=1, tiled=True),
        lax.psum_scatter(gradients[4][None], "cam", scatter_dimension=1, tiled=True),
        lax.psum_scatter(gradients[5][None], "cam", scatter_dimension=1, tiled=True),
    )
    per_device = ray_total // lax.axis_size("depth")
    pixel_out = lax.dynamic_slice_in_dim(
        pixels, lax.axis_index("depth") * per_device, per_device, 0
    )[None]
    return (pixel_out, reduced[0], reduced[1], reduced[2], reduced[3], reduced[4], reduced[5])


def solution(mesh):
    placed = (
        P("depth", "cam", None),
        P("depth", "cam", None),
        P("cam"),
        P("cam", None, None),
        P("cam", None, None),
        P("depth", None, None),
        P("depth", None, None),
        P("depth", None),
        P("depth", None, None),
        P("depth", None),
        P("depth", None, None),
        P("depth", None),
    )
    return jax.shard_map(
        shards,
        mesh=mesh,
        in_specs=placed,
        out_specs=(
            P("cam", "depth", None),
            P("depth", "cam", None),
            P("depth", "cam"),
            P("depth", "cam", None),
            P("depth", "cam"),
            P("depth", "cam", None),
            P("depth", "cam"),
        ),
        check_vma=False,
    )
```

profile of v0, /device:TPU:1, one launch (start us, length us, event | category | flops | bytes accessed | tf_op | source)
XLA Modules:
  0.0 497.7 jit_solution(9353184948084471746)
XLA Ops:
  7.9 1.2 fusion.40
  13.0 4.0 sine_convert_fusion
  17.0 1.7 fusion.7
  24.4 20.8 %all-gather.2 = f32[16,1,128]{2,1,0:T(1,128)S(1)} all-gather(f32[1,1,128]{2,1,0:T(1,128)S(1)} %get-tuple-element.230), channel_id=3, replica_groups=mesh['depth'=16,'cam'=32] {'depth'}, dimensions={0}, use_global_device_ids=true | all-gather | bytes 8704 | tf_op jit(solution)/shard_map/all_gather | solution.py:16
  46.0 1.7 fusion.54
  48.5 20.5 %all-gather = f32[2048,64]{1,0:T(8,128)} all-gather(f32[128,64]{1,0:T(8,128)S(1)} %scatter_custom_fusion), channel_id=2, replica_groups=mesh['depth'=16,'cam'=32] {'depth'}, dimensions={0}, use_global_device_ids=true | all-gather | bytes 557056 | tf_op jit(solution)/shard_map/all_gather | solution.py:16
  69.0 1.0 while.27
  69.0 1.0 fusion.81
  71.1 30.6 %while.26 = (s32[]{:T(128)}, f32[128,64]{1,0:T(8,128)S(1)}, f32[128]{0:T(128)}, s32[]{:T(128)}, pred[]{:T(512)}, /*index=5*/f32[16,128,64]{2,1,0:T(8,128)}, f32[...) while((s32[]{:T(128)}, f32[128,64]{1,0:T(8,128)S(1)}, f32[128]{0:T(128)}, s32[]{:T(128)}, ...), condition=%wide.region_3.4_spmd, body=%wide.region_2.3_spmd.sunk | while | flops 41094 | bytes 102572 | solution.py:25
  71.8 1.0 fusion.79
  74.0 1.0 fusion.79
  76.2 1.0 fusion.79
  78.4 1.0 fusion.79
  80.6 1.0 fusion.79
  95.9 1.0 fusion.79
  98.1 1.0 fusion.79
  100.3 1.0 fusion.79
  101.8 1.4 multiply_reduce_fusion
  107.1 1.6 multiply_convert_fusion
  108.7 1.0 fusion.55
  110.7 1.4 fusion.56
  112.3 1.3 convert_reduce_fusion
  113.9 1.0 convert_reduce_fusion.1
  115.6 1.1 convolution_bitcast_fusion.1
  116.8 3.7 convolution_bitcast_fusion
  120.5 1.3 dynamic-slice
  123.4 63.8 %all-reduce.5 = (f32[1,256]{1,0:T(1,128)S(1)}, f32[1,256]{1,0:T(1,128)S(1)}, f32[1,256]{1,0:T(1,128)S(1)}) all-reduce(f32[1,256]{1,0:T(1,128)S(1)} %bitcast.178, f32[1,256]{1,0:T(1,128)S(1)} %bitcast.177, f32[1,256]{1,0:T(1,128)S(1)} %fusion.57), channel_id=5, replica_groups=mesh['depth'=16,'cam'=32] {'cam'}, use_global_device_ids=true, to_apply=%region_9.10.clone | all-reduce | flops 768 | bytes 6144
  188.4 1.3 dynamic-slice_bitcast_fusion.2
  189.7 76.9 %all-reduce.9.cloned.1.call-done = (f32[1,128,256]{2,1,0:T(8,128)}, f32[1,256,64]{2,0,1:T(1,128)}) async-done(((f32[1,128,256]{2,1,0:T(8,128)}, f32[1,256,64]{2,0,1:T(1,128)}), (f32[1,128,256]{2,1,0:T(8,128)}, f32[1,256,64]{2,0,1:T(1,128)})) %all-reduce.9.cloned.1.call-update) | async-done | bytes 196624
  266.6 1.3 constant_dynamic-slice_fusion.1
  267.8 1.3 constant_dynamic-slice_fusion.4
  269.1 221.7 %reduce-scatter.6.cloned.1.call-done = f32[1,8,256]{2,1,0:T(8,128)} async-done(((f32[1,256,256]{2,1,0:T(8,128)}), f32[1,8,256]{2,1,0:T(8,128)}) %reduce-scatter.6.cloned.1.call-update) | async-done | bytes 8208 | tf_op jit(solution)/shard_map/reduce_scatter | solution.py:186
  (137 shorter events, 42.6 us)
Async XLA Ops:
  7.2 11.6 %copy-start = (bf16[1,256,256]{2,1,0:T(8,128)(2,1)S(1)}, bf16[1,256,256]{2,1,0:T(8,128)(2,1)}, u32[]{:S(2)}) copy-start(bf16[1,256,256]{2,1,0:T(8,128)(2,1)} %param.24) | copy-start | bytes 393220
  7.2 259.4 %all-reduce.9.cloned.1.call-start = ((), (), s32[]{:S(2)}) async-start(), calls=%async_computation.2 | async-start | bytes 524288
  9.1 3.9 copy-start.22
  10.5 0.6 copy-start.8
  11.1 1.8 copy-start.20
  17.0 1.7 copy-start.2
  17.0 1.7 copy-start.4
  17.0 1.8 copy-start.23
  18.7 1.4 copy-start.25
  18.7 1.3 copy-start.21
  20.1 2.1 copy-start.18
  20.1 25.2 %copy-start.16 = (bf16[1,256,64]{1,2,0:T(8,128)(2,1)S(1)}, bf16[1,256,64]{1,2,0:T(8,128)(2,1)}, u32[]{:S(2)}) copy-start(bf16[1,256,64]{1,2,0:T(8,128)(2,1)} %param.26) | copy-start | bytes 98308
  20.7 27.0 %copy-start.6 = (f32[1,4096]{1,0:T(1,128)}, f32[1,4096]{1,0:T(1,128)S(1)}, u32[]{:S(2)}) copy-start(f32[1,4096]{1,0:T(1,128)S(1)} %fusion.38) | copy-start | bytes 49156
  20.9 26.9 %copy-start.12 = (f32[32,128]{1,0:T(8,128)}, f32[32,128]{1,0:T(8,128)S(1)}, u32[]{:S(2)}) copy-start(f32[32,128]{1,0:T(8,128)S(1)} %fusion.20) | copy-start | bytes 49156
  20.9 26.8 %copy-start.10 = (f32[32,128]{1,0:T(8,128)}, f32[32,128]{1,0:T(8,128)S(1)}, u32[]{:S(2)}) copy-start(f32[32,128]{1,0:T(8,128)S(1)} %fusion.30) | copy-start | bytes 49156
  70.0 0.6 copy-start.14
  70.0 0.6 copy-start.19
  103.2 6.6 %copy-start.9 = (s32[32,1]{1,0:T(8,128)S(1)}, s32[32,1]{1,0:T(8,128)}, u32[]{:S(2)}) copy-start(s32[32,1]{1,0:T(8,128)} %copy-done.8) | copy-start | bytes 388
  103.2 6.6 %copy-start.11 = (f32[32,128]{1,0:T(8,128)S(1)}, f32[32,128]{1,0:T(8,128)}, u32[]{:S(2)}) copy-start(f32[32,128]{1,0:T(8,128)} %copy-done.10) | copy-start | bytes 49156
  103.2 6.6 %copy-start.13 = (f32[32,128]{1,0:T(8,128)S(1)}, f32[32,128]{1,0:T(8,128)}, u32[]{:S(2)}) copy-start(f32[32,128]{1,0:T(8,128)} %copy-done.12) | copy-start | bytes 49156
  103.2 6.8 %copy-start.15 = (f32[4096]{0:T(1024)S(1)}, f32[4096]{0:T(1024)}, u32[]{:S(2)}) copy-start(f32[4096]{0:T(1024)} %get-tuple-element.222) | copy-start | bytes 49156
  110.0 2.1 copy-start.7
  110.0 2.3 copy-start.1
  110.1 2.3 copy-start.17
  110.1 2.3 copy-start.24
  112.3 1.6 copy-start.26
  113.6 1.3 copy-start.27
  113.9 1.4 copy-start.3
  113.9 1.6 copy-start.5
  116.7 374.1 %reduce-scatter.6.cloned.1.call-start = ((), (), s32[]{:S(2)}) async-start(), calls=%async_computation.1 | async-start | bytes 270336 | tf_op jit(solution)/shard_map/reduce_scatter | solution.py:186
Sparse Core Ops, SparseCore 0:
  116.9 149.6 all-reduce.8
  271.5 219.2 reduce-scatter.5
where the time goes:
time: 504 us; the launch traced here: 498 us
  waiting for transfers between devices  299 us (59%)
  blocking collectives  105 us (21%)
  other arithmetic  41 us (8%)
  local copies, waits for them, and re-layouts  20.6 us (4%)
  between operations  16.4 us (3%)
  matrix products  15.8 us (3%)
    reduce_scatter x1, waiting for transfers between devices, shards(): lax.psum_scatter(gradients[2][None], 'cam', scatter_dimension=1, tiled=True)  222 us
    unnamed x3, waiting for transfers between devices  76.9 us
    unnamed x1, blocking collectives  63.8 us
    all_gather x2, blocking collectives, carried_in(): gathered = jax.tree.map(lambda a: lax.all_gather(a, axis), part)  41.3 us
    select_n x15, other arithmetic, join_pairs(): return (jnp.where(descending, falling, rising), low_through * high_through)  14.4 us
    mul x16, other arithmetic, join_pairs(): return (jnp.where(descending, falling, rising), low_through * high_through)  10.5 us
  transfers between devices with their start and end apart: 2, of which 2 were waited for; matrix products, arithmetic and copies ran while one was open for 2% of the time, Pallas kernels for 0%

commit v1 on v0

v1 whole, which is shorter than its diff:
```python
import functools
import math

import jax
import jax.numpy as jnp
from jax import lax
from jax.experimental import pallas as pl
from jax.experimental.pallas import tpu as pltpu
from jax.sharding import PartitionSpec as P

BLK = 128
CAP = 32
RAYS = 128
FEAT = 64
HID = 256
ENC = 128
REGIONS = 16
BATCHES = 32
CHUNK = 4
ROWS = CHUNK * BLK
STEP = 1.0 / 64.0
F32 = jnp.float32
BF16 = jnp.bfloat16
HIGH = lax.Precision.HIGHEST

TURN_HIGH = 6.28125
TURN_LOW = 2.0 * math.pi - 6.28125
SINE = (
    0.999999994451582,
    -0.16666664569587258,
    0.008333310299565085,
    -0.00019840151845895466,
    2.752938860313289e-06,
    -2.4676381628551014e-08,
    1.3449464950123382e-10,
)


def nn(a, b):
    return lax.dot_general(a, b, (((1,), (0,)), ((), ())), preferred_element_type=F32)


def nt(a, b, precision=None):
    return lax.dot_general(
        a, b, (((1,), (1,)), ((), ())), preferred_element_type=F32, precision=precision
    )


def tn(a, b):
    return lax.dot_general(a, b, (((0,), (0,)), ((), ())), preferred_element_type=F32)


def sine_of(angle, shift):
    turns = jnp.floor(angle * (0.5 / math.pi) + (shift + 0.5))
    rest = (angle - turns * TURN_HIGH) - turns * TURN_LOW + shift * (2.0 * math.pi)
    square = rest * rest
    value = jnp.full_like(rest, SINE[-1])
    for coefficient in SINE[-2::-1]:
        value = value * square + coefficient
    return value * rest


def forward_kernel(
    rays,
    offsets,
    frames,
    freq,
    w_in,
    b_in,
    w_mid,
    b_mid,
    w_heads,
    payload,
    encoded,
    hidden_one,
    hidden_two,
    kept,
    anchor,
    slope,
    heads,
    dens,
):
    lane = lax.broadcasted_iota(jnp.int32, (BLK, 128), 1)
    columns = jnp.concatenate([frames[...], jnp.zeros((2, RAYS), F32)], axis=0).T
    both = jnp.concatenate([freq[...], freq[...]], axis=1)
    anchor[...] = (
        columns[:, 0:1] * both[0:1] + columns[:, 1:2] * both[1:2] + columns[:, 2:3] * both[2:3]
    )
    slope[...] = (
        columns[:, 3:4] * both[0:1] + columns[:, 4:5] * both[1:2] + columns[:, 5:6] * both[2:3]
    )
    dens[...] = jnp.zeros_like(dens)

    rows = lax.broadcasted_iota(jnp.int32, (24, 128), 0)
    cols = lax.broadcasted_iota(jnp.int32, (24, 128), 1)
    low_half = cols < FEAT
    shift = jnp.where(low_half, 0.0, 0.25).astype(F32)
    coarse = rows < 16
    coarse_steps = jnp.where(coarse, 8 * rows, rows - 16).astype(F32)
    sign = jnp.where(low_half[:16], 1.0, -1.0).astype(F32)

    def encode(slot):
        ray = jnp.maximum(rays[slot], 0)
        start = offsets[slot].astype(F32) + 0.5
        base = anchor[pl.ds(ray, 1), :]
        direction = slope[pl.ds(ray, 1), :]
        times = (coarse_steps + jnp.where(coarse, start, 0.0)) * STEP
        angle = jnp.where(coarse, base, 0.0) + times * direction
        table = sine_of(angle, shift)
        swapped = pltpu.roll(table, 64, 1)
        sine_cosine = table[:16]
        quarter_on = swapped[:16] * sign
        fine, fine_swapped = table[16:], swapped[16:]
        fine_sine = jnp.where(low_half[:8], fine, fine_swapped)
        fine_cosine = jnp.where(low_half[:8], fine_swapped, fine)
        parts = [
            sine_cosine[i : i + 1] * fine_cosine + quarter_on[i : i + 1] * fine_sine
            for i in range(16)
        ]
        return jnp.concatenate(parts, axis=0).astype(BF16)

    def chunk(step, carry):
        start = pl.multiple_of(step * ROWS, ROWS)
        enc = jnp.concatenate([encode(step * CHUNK + q) for q in range(CHUNK)], axis=0)
        encoded[pl.ds(start, ROWS), :] = enc
        one = jnp.maximum(nn(enc, w_in[...]) + b_in[...], 0.0).astype(BF16)
        hidden_one[pl.ds(start, ROWS), :] = one
        two = jnp.maximum(nn(one, w_mid[...]) + b_mid[...], 0.0).astype(BF16)
        hidden_two[pl.ds(start, ROWS), :] = two
        both_heads = nn(two, w_heads[...])
        heads[pl.ds(start, ROWS), :] = both_heads
        taken = dens[...]
        for q in range(CHUNK):
            taken = jnp.where(
                lane == FEAT + step * CHUNK + q, both_heads[q * BLK : (q + 1) * BLK], taken
            )
        dens[...] = taken
        return carry

    lax.fori_loop(0, CAP // CHUNK, chunk, 0)

    pre = pltpu.roll(dens[...], 64, 1)
    tau = (jnp.maximum(pre, 0.0) + jnp.log1p(jnp.exp(-jnp.abs(pre)))) * STEP
    row_index = lax.broadcasted_iota(jnp.int32, (BLK, BLK), 0)
    earlier = (lane < row_index).astype(F32)
    before = lax.dot_general(
        earlier, tau, (((1,), (0,)), ((), ())), preferred_element_type=F32, precision=HIGH
    )
    series = tau * (1.0 - tau * (0.5 - tau * (1.0 / 6.0 - tau * (1.0 / 24.0))))
    opacity = jnp.where(tau < 0.03, series, 1.0 - jnp.exp(-tau))
    weight = jnp.exp(-before) * opacity
    passed = jnp.exp(-(before + tau))
    kept[0] = weight
    kept[1] = passed
    kept[2] = jax.nn.sigmoid(pre) * STEP
    last = 1.0 - passed[BLK - 1 : BLK, :]
    lane_row = lane[0:1]
    for slot in range(CAP):
        colour = jnp.sum(
            weight[:, slot : slot + 1] * heads[slot * BLK : (slot + 1) * BLK, :],
            axis=0,
            keepdims=True,
        )
        row = jnp.where(lane_row < FEAT, colour, last[:, slot : slot + 1])
        row = jnp.where(lane_row == 127, rays[slot].astype(F32), row)
        payload[slot : slot + 1, :] = row


def backward_kernel(
    rays,
    place,
    order,
    gathered,
    target,
    w_heads,
    w_mid,
    encoded,
    hidden_one,
    hidden_two,
    kept,
    pixels,
    packed,
    chosen,
    aim,
    slopes,
    proj,
    pre_grad,
    sum_feat,
    sum_mid,
    sum_in,
    bias_mid,
    bias_in,
):
    region = place[0]
    descending = order[0] == 1
    lane = lax.broadcasted_iota(jnp.int32, (BLK, 128), 1)

    own = gathered[region]
    wanted = jnp.concatenate(
        [
            own[:, 127:128],
            (lax.broadcasted_iota(jnp.int32, (8, 1), 0) + 8 * region).astype(F32),
        ],
        axis=0,
    )
    picker = (lax.broadcasted_iota(jnp.int32, (8, 128), 1) == 127).astype(F32)
    group_of = lax.broadcasted_iota(jnp.int32, (40, 128), 1) // CAP
    for group in range(4):
        rows = gathered[4 * group : 4 * group + 4].reshape(128, 128)
        names = nt(picker, rows, HIGH)[0:1]
        same = wanted == names
        left = jnp.concatenate(
            [
                jnp.where(same & (group_of == k), 1.0, 0.0).astype(BF16)
                for k in range(4)
            ],
            axis=0,
        )
        first = rows.astype(BF16)
        rest = rows - first.astype(F32)
        second = rest.astype(BF16)
        third = (rest - second.astype(F32)).astype(BF16)
        found = (nn(left, third) + nn(left, second)) + nn(left, first)
        chosen[4 * group : 4 * group + 4] = found.reshape(4, 40, 128)

    position = jnp.where(descending, REGIONS - 1 - region, region)
    total = jnp.zeros((40, 128), F32)
    through = jnp.ones((40, 128), F32)
    near = jnp.ones((40, 128), F32)
    far = jnp.zeros((40, 128), F32)
    far_through = jnp.ones((40, 128), F32)
    for step in range(REGIONS):
        source = jnp.where(descending, REGIONS - 1 - step, step)
        here = chosen[source]
        through_here = 1.0 - jnp.broadcast_to(here[:, FEAT : FEAT + 1], (40, 128))
        total = total + through * here
        near = jnp.where(step < position, near * through_here, near)
        beyond = step > position
        far = jnp.where(beyond, far + far_through * here, far)
        far_through = jnp.where(beyond, far_through * through_here, far_through)
        through = through * through_here
    pixels[...] = total[32:40, :FEAT]

    for slot in range(CAP):
        slopes[slot : slot + 1, :FEAT] = target[pl.ds(jnp.maximum(rays[slot], 0), 1), :]
    occupied = (own[:, 127:128] >= 0.0) & (lane[:CAP] < FEAT)
    scaled = jnp.where(occupied, near[:CAP] * (total[:CAP] - slopes[...]), 0.0)
    inner = jnp.where(occupied, scaled * far[:CAP], 0.0)
    slopes[...] = scaled
    blank = jnp.zeros((96, 128), F32)
    d_through = nt(jnp.ones((8, 128), F32), jnp.concatenate([inner, blank], axis=0), HIGH)[0:1]
    twice = jnp.concatenate([scaled, scaled, blank[:64]], axis=0)
    direction = nt(w_heads[...].astype(F32), twice, HIGH)
    upper = direction.astype(BF16)
    lower = (direction - upper.astype(F32)).astype(BF16)
    lane_hid = lax.broadcasted_iota(jnp.int32, (HID, 128), 1)
    aim[...] = jnp.where(lane_hid < CAP, upper.astype(F32), lower.astype(F32)).astype(BF16)

    proj[...] = jnp.zeros_like(proj)
    slot_lane = jnp.where(lane < 2 * CAP, lane & (CAP - 1), -1)

    def project(step, carry):
        start = pl.multiple_of(step * ROWS, ROWS)
        part = nn(hidden_two[pl.ds(start, ROWS), :], aim[...])
        taken = proj[...]
        for q in range(CHUNK):
            taken = jnp.where(
                slot_lane == step * CHUNK + q, part[q * BLK : (q + 1) * BLK], taken
            )
        proj[...] = taken
        return carry

    lax.fori_loop(0, CAP // CHUNK, project, 0)
    projected = proj[...] + pltpu.roll(proj[...], 96, 1)
    row_index = lax.broadcasted_iota(jnp.int32, (BLK, BLK), 0)
    later = (lane > row_index).astype(F32)
    weight, passed = kept[0], kept[1]
    behind = lax.dot_general(
        later,
        projected * weight,
        (((1,), (0,)), ((), ())),
        preferred_element_type=F32,
        precision=HIGH,
    )
    d_tau = projected * passed - behind - d_through * passed[BLK - 1 : BLK, :]
    pre_grad[...] = d_tau * kept[2]

    for ref in (sum_feat, sum_mid, sum_in, bias_mid, bias_in):
        ref[...] = jnp.zeros_like(ref)

    def chunk(step, carry):
        start = pl.multiple_of(step * ROWS, ROWS)
        turn = lax.rem(128 - step * CHUNK, 128)
        weights = pltpu.roll(kept[0], turn, 1)
        pres = pltpu.roll(pre_grad[...], turn, 1)
        parts = []
        for q in range(CHUNK):
            colour = slopes[pl.ds(step * CHUNK + q, 1), :]
            pre_here = jnp.where(lane == FEAT, pres[:, q : q + 1], 0.0)
            parts.append(jnp.where(lane < FEAT, weights[:, q : q + 1] * colour, pre_here))
        d_heads = jnp.concatenate(parts, axis=0).astype(BF16)
        two = hidden_two[pl.ds(start, ROWS), :]
        one = hidden_one[pl.ds(start, ROWS), :]
        enc = encoded[pl.ds(start, ROWS), :]
        sum_feat[...] += tn(two, d_heads)
        d_two = jnp.where(two.astype(F32) > 0.0, nt(d_heads, w_heads[...]), 0.0)
        bias_mid[...] += jnp.sum(d_two.reshape(ROWS // 8, 8, HID), axis=0)
        d_two = d_two.astype(BF16)
        sum_mid[...] += tn(one, d_two)
        d_one = jnp.where(one.astype(F32) > 0.0, nt(d_two, w_mid[...]), 0.0)
        bias_in[...] += jnp.sum(d_one.reshape(ROWS // 8, 8, HID), axis=0)
        sum_in[...] += tn(enc, d_one.astype(BF16))
        return carry

    lax.fori_loop(0, CAP // CHUNK, chunk, 0)

    spread = jnp.concatenate(
        [
            jnp.zeros((96, HID), F32),
            jnp.broadcast_to(jnp.sum(bias_in[...], axis=0, keepdims=True), (8, HID)),
            jnp.broadcast_to(jnp.sum(bias_mid[...], axis=0, keepdims=True), (24, HID)),
        ],
        axis=0,
    ).T
    sum_feat[...] = jnp.where(lane_hid < 96, sum_feat[...], spread)
    for part in range(BATCHES):
        packed[part, 0:8, :] = sum_mid[8 * part : 8 * part + 8, 0:128]
        packed[part, 8:16, :] = sum_mid[8 * part : 8 * part + 8, 128:256]
        packed[part, 16:20, :] = sum_in[4 * part : 4 * part + 4, 0:128]
        packed[part, 20:24, :] = sum_in[4 * part : 4 * part + 4, 128:256]
        packed[part, 24:32, :] = sum_feat[8 * part : 8 * part + 8, :]


def finish_kernel(parts, g_in, gb_in, g_mid, gb_mid, g_feat, g_dens):
    total = jnp.sum(parts[...], axis=0)
    g_mid[:, 0:128] = total[0:8]
    g_mid[:, 128:256] = total[8:16]
    g_in[:, 0:128] = total[16:20]
    g_in[:, 128:256] = total[20:24]
    g_feat[...] = total[24:32, :FEAT]
    turned = jnp.concatenate([total[24:32], jnp.zeros((120, 128), F32)], axis=0).T
    g_dens[...] = turned[FEAT : FEAT + 1, 0:8]
    gb_in[...] = turned[96:97, 0:8]
    gb_mid[...] = turned[104:105, 0:8]


VMEM = pl.BlockSpec(memory_space=pltpu.VMEM)
SMEM = pl.BlockSpec(memory_space=pltpu.SMEM)


def shards(
    block_rays,
    block_offsets,
    view_order,
    ray_frames,
    target,
    enc_freq,
    w_in,
    b_in,
    w_mid,
    b_mid,
    w_feat,
    w_dens,
):
    samples = CAP * BLK
    slot_rays = block_rays.reshape(CAP)
    slot_offsets = block_offsets.reshape(CAP)
    w_heads = jnp.concatenate(
        [w_feat[0], jnp.broadcast_to(w_dens[0][:, None], (HID, 128 - FEAT))], axis=1
    )
    payload, encoded, hidden_one, hidden_two, kept = pl.pallas_call(
        forward_kernel,
        name="forward",
        out_shape=(
            jax.ShapeDtypeStruct((CAP, 128), F32),
            jax.ShapeDtypeStruct((samples, ENC), BF16),
            jax.ShapeDtypeStruct((samples, HID), BF16),
            jax.ShapeDtypeStruct((samples, HID), BF16),
            jax.ShapeDtypeStruct((3, BLK, 128), F32),
        ),
        in_specs=[SMEM, SMEM] + [VMEM] * 7,
        out_specs=(VMEM,) * 5,
        scratch_shapes=[
            pltpu.VMEM((RAYS, 128), F32),
            pltpu.VMEM((RAYS, 128), F32),
            pltpu.VMEM((samples, 128), F32),
            pltpu.VMEM((BLK, 128), F32),
        ],
    )(
        slot_rays,
        slot_offsets,
        ray_frames[0],
        enc_freq[0],
        w_in[0],
        b_in,
        w_mid[0],
        b_mid,
        w_heads,
    )
    gathered = lax.all_to_all(
        jnp.broadcast_to(payload[None], (REGIONS, CAP, 128)), "depth", 0, 0, tiled=True
    )
    place = lax.axis_index("depth").astype(jnp.int32).reshape(1)
    pixels, packed = pl.pallas_call(
        backward_kernel,
        name="backward",
        out_shape=(
            jax.ShapeDtypeStruct((8, FEAT), F32),
            jax.ShapeDtypeStruct((BATCHES, 32, 128), F32),
        ),
        in_specs=[SMEM] * 3 + [VMEM] * 8,
        out_specs=(VMEM,) * 2,
        scratch_shapes=[
            pltpu.VMEM((REGIONS, 40, 128), F32),
            pltpu.VMEM((HID, 128), BF16),
            pltpu.VMEM((CAP, 128), F32),
            pltpu.VMEM((BLK, 128), F32),
            pltpu.VMEM((BLK, 128), F32),
            pltpu.VMEM((HID, 128), F32),
            pltpu.VMEM((HID, HID), F32),
            pltpu.VMEM((ENC, HID), F32),
            pltpu.VMEM((8, HID), F32),
            pltpu.VMEM((8, HID), F32),
        ],
    )(
        slot_rays,
        place,
        view_order,
        gathered,
        target[0],
        w_heads,
        w_mid[0],
        encoded,
        hidden_one,
        hidden_two,
        kept,
    )
    received = lax.all_to_all(packed, "cam", 0, 0, tiled=True)
    g_in, gb_in, g_mid, gb_mid, g_feat, g_dens = pl.pallas_call(
        finish_kernel,
        name="finish",
        out_shape=(
            jax.ShapeDtypeStruct((4, HID), F32),
            jax.ShapeDtypeStruct((1, 8), F32),
            jax.ShapeDtypeStruct((8, HID), F32),
            jax.ShapeDtypeStruct((1, 8), F32),
            jax.ShapeDtypeStruct((8, FEAT), F32),
            jax.ShapeDtypeStruct((1, 8), F32),
        ),
        in_specs=[VMEM],
        out_specs=(VMEM,) * 6,
    )(received)
    return (pixels[None], g_in[None], gb_in, g_mid[None], gb_mid, g_feat[None], g_dens)


def solution(mesh):
    placed = (
        P("depth", "cam", None),
        P("depth", "cam", None),
        P("cam"),
        P("cam", None, None),
        P("cam", None, None),
        P("depth", None, None),
        P("depth", None, None),
        P("depth", None),
        P("depth", None, None),
        P("depth", None),
        P("depth", None, None),
        P("depth", None),
    )
    return jax.shard_map(
        shards,
        mesh=mesh,
        in_specs=placed,
        out_specs=(
            P("cam", "depth", None),
            P("depth", "cam", None),
            P("depth", "cam"),
            P("depth", "cam", None),
            P("depth", "cam"),
            P("depth", "cam", None),
            P("depth", "cam"),
        ),
        check_vma=False,
    )
```

time: 504 us -> 83.4 us (0.17); the launches traced: 498 us -> 82.8 us
  waiting for transfers between devices: 299 us -> 9.62 us
  blocking collectives: 105 us -> 27.7 us
  other arithmetic: 41 us -> 1.42 us
  Pallas kernels: 0 us -> 25.5 us
  matrix products: 15.8 us -> 0 us
  between operations: 16.4 us -> 1.3 us
  local copies, waits for them, and re-layouts: 20.6 us -> 7.12 us
  starting transfers between devices: 0.08 us -> 10.2 us
    reduce_scatter x1 -> x0, waiting for transfers between devices: 222 us -> none  [shards(): lax.psum_scatter(gradients[2][None], 'cam', scatter_dimension=1, tiled=True)]
    unnamed x3 -> x0, waiting for transfers between devices: 76.9 us -> none
    unnamed x1 -> x0, blocking collectives: 63.8 us -> none
    all_gather x2 -> x0, blocking collectives: 41.3 us -> none  [carried_in(): gathered = jax.tree.map(lambda a: lax.all_gather(a, axis), part)]
    all_to_all x0 -> x1, blocking collectives: none -> 27.7 us  [shards(): received = lax.all_to_all(packed, 'cam', 0, 0, tiled=True)]
    pallas_call x0 -> x3, Pallas kernels: none -> 25.5 us  [the longest x1 14.3 us: shards(): pl.pallas_call(backward_kernel, name='backward', out_shape=(jax.ShapeDtyp...]
    dot_general x14 -> x0, matrix products: 15.8 us -> none  [the longest x3 6.19 us: contract_rows(): lax.dot_general(left, right, (((0,), (0,)), ((), ())), preferred_element_...]
    select_n x16 -> x0, other arithmetic: 14.5 us -> none  [the longest x15 14.4 us: join_pairs(): return (jnp.where(descending, falling, rising), low_through * high_through)]
  transfers between devices with their start and end apart: 2 -> 1, of which waited for: 2 -> 1; matrix products, arithmetic and copies ran while one was open for 2% -> 2% of each run, Pallas kernels for 0% -> 0%
where the time goes in v1:
time: 83.4 us; the launch traced here: 82.8 us
  blocking collectives  27.7 us (33%)
  Pallas kernels  25.5 us (31%)
  starting transfers between devices  10.2 us (12%)
  waiting for transfers between devices  9.62 us (12%)
  local copies, waits for them, and re-layouts  7.12 us (9%)
  other arithmetic  1.42 us (2%)
  between operations  1.3 us (2%)
    all_to_all x1, blocking collectives, shards(): received = lax.all_to_all(packed, 'cam', 0, 0, tiled=True)  27.7 us
    pallas_call x1, Pallas kernels, shards(): pl.pallas_call(backward_kernel, name='backward', out_shape=(jax.ShapeDtyp...  14.3 us
    all_to_all x1, starting transfers between devices, shards(): lax.all_to_all(jnp.broadcast_to(payload[None], (REGIONS, CAP, 128)), 'dep...  10.2 us
    all_to_all x1, waiting for transfers between devices, shards(): lax.all_to_all(jnp.broadcast_to(payload[None], (REGIONS, CAP, 128)), 'dep...  9.62 us
    pallas_call x1, Pallas kernels, shards(): pl.pallas_call(forward_kernel, name='forward', out_shape=(jax.ShapeDtypeS...  9.45 us
    unnamed x6, local copies, waits for them, and re-layouts  5.59 us
    pallas_call x1, Pallas kernels, shards(): pl.pallas_call(finish_kernel, name='finish', out_shape=(jax.ShapeDtypeStr...  1.78 us
  transfers between devices with their start and end apart: 1, of which 1 were waited for; matrix products, arithmetic and copies ran while one was open for 2% of the time, Pallas kernels for 0%

profile of v1, /device:TPU:1, one launch (start us, length us, event | category | flops | bytes accessed | tf_op | source)
XLA Modules:
  0.0 82.8 jit_solution(1994301893238092890)
XLA Ops:
  0.6 1.3 %copy.26 = f32[1,3,64]{2,1,0:T(4,128)} copy(f32[1,3,64]{2,0,1:T(1,128)} %param.17) | data formatting | bytes 1536
  1.9 1.3 %copy.25 = f32[1,6,128]{2,1,0:T(8,128)} copy(f32[1,6,128]{2,0,1:T(1,128)} %param.15) | data formatting | bytes 6144
  3.2 0.9 %copy.19 = bf16[1,256,64]{2,1,0:T(8,128)(2,1)S(1)} copy(bf16[1,256,64]{1,2,0:T(8,128)(2,1)} %param.22) | data formatting | bytes 65536 | tf_op args[10]
  4.0 0.7 reduce
  4.7 0.1 broadcast_in_dim.26
  4.9 0.7 pad_maximum_fusion.w_heads
  5.6 9.5 %forward.1 = (f32[32,128]{1,0:T(8,128)}, bf16[4096,128]{1,0:T(8,128)(2,1)}, bf16[4096,256]{1,0:T(8,128)(2,1)}, bf16[4096,256]{1,0:T(8,128)(2,1)}, f32[3,128,128]{2,1,0:T(8,128)}) custom-call(s32[32]{0:T(128)} %bitcast.24, s32[32]{0:T(128)} %bitcast.26, f32[6,128]{1,0:T(8,128)} %bitcast.22, f32[3,64]{1,0:T(4,128)} %bitcast.23, bf16[128,256]{1,0:T(8,128)(2,1)} %bitcast.21, ...), custom_call_target="tpu_custom_call" | custom-call | tf_op jit(solution)/shard_map/forward/pallas_call | solution.py:371
  15.0 1.4 %broadcast_in_dim.27 = f32[16,32,128]{2,1,0:T(8,128)} broadcast(f32[32,128]{1,0:T(8,128)} %get-tuple-element.20), dimensions={1,2} | broadcast | bytes 278528 | tf_op jit(solution)/shard_map/broadcast_in_dim | solution.py:401
  16.4 10.2 %all-to-all-start = ((f32[16,32,128]{2,1,0:T(8,128)}), f32[16,32,128]{2,1,0:T(8,128)S(1)}, u32[]{:S(2)}, u32[]{:S(2)}) async-start(f32[16,32,128]{2,1,0:T(8,128)} %broadcast_in_dim.27), calls=%async_computation | async-start | bytes 524288 | tf_op jit(solution)/shard_map/all_to_all | solution.py:400
  27.3 1.5 %copy.20 = f32[1,128,64]{2,1,0:T(8,128)} copy(f32[1,128,64]{1,2,0:T(8,128)} %param.16) | data formatting | bytes 65536 | tf_op args[4]
  28.7 9.6 %all-to-all-done.gathered = f32[16,32,128]{2,1,0:T(8,128)S(1)} async-done(((f32[16,32,128]{2,1,0:T(8,128)}), f32[16,32,128]{2,1,0:T(8,128)S(1)}, u32[]{:S(2)}, u32[]{:S(2)}) %all-to-all-start) | async-done | bytes 262176 | tf_op jit(solution)/shard_map/all_to_all | solution.py:400
  38.4 0.0 copy-start
  38.4 0.7 copy-done
  39.1 14.3 %backward.1 = (f32[8,64]{1,0:T(8,128)}, f32[32,32,128]{2,1,0:T(8,128)}) custom-call(s32[32]{0:T(128)} %bitcast.25, s32[1]{0:T(128)} %bitcast.1.place, s32[1]{0:T(128)S(6)} %copy.27.order, f32[16,32,128]{2,1,0:T(8,128)} %copy-done, f32[128,64]{1,0:T(8,128)} %bitcast.20, bf16[256,128]{1,0:T(8,128)(2,1)} %pad_maximum_fusion.w_heads, bf16[256,256]{1,0:T(8,128)(2,1)} %bitcast.18, ...), custom_call_target="tpu_custom_call" | custom-call | tf_op jit(solution)/shard_map/backward/pallas_call | solution.py:404
  53.4 27.7 %all_to_all.10.parts = f32[32,32,128]{2,1,0:T(8,128)} all-to-all(f32[32,32,128]{2,1,0:T(8,128)} %get-tuple-element.26), channel_id=1, replica_groups=mesh['depth'=16,'cam'=32] {'cam'}, dimensions={0} | all-to-all | bytes 1048576 | tf_op jit(solution)/shard_map/all_to_all | solution.py:438
  81.1 1.8 %finish.1 = (f32[4,256]{1,0:T(4,128)}, f32[1,8]{1,0:T(1,128)}, f32[8,256]{1,0:T(8,128)}, f32[1,8]{1,0:T(1,128)}, f32[8,64]{1,0:T(8,128)}, /*index=5*/f32[1,8]{1,0:T(1,128)}) custom-call(f32[32,32,128]{2,1,0:T(8,128)} %all_to_all.10.parts), custom_call_target="tpu_custom_call" | custom-call | tf_op jit(solution)/shard_map/finish/pallas_call | solution.py:439
Async XLA Ops:
  16.4 21.9 %all-to-all-start = ((f32[16,32,128]{2,1,0:T(8,128)}), f32[16,32,128]{2,1,0:T(8,128)S(1)}, u32[]{:S(2)}, u32[]{:S(2)}) async-start(f32[16,32,128]{2,1,0:T(8,128)} %broadcast_in_dim.27), calls=%async_computation | async-start | bytes 524288 | tf_op jit(solution)/shard_map/all_to_all | solution.py:400
  38.4 0.7 copy-start

commit v2 on v1

--- a/solution.py
+++ b/solution.py
@@ -50,6 +50,13 @@
     return lax.dot_general(a, b, (((0,), (0,)), ((), ())), preferred_element_type=F32)
 
 
+def thirds(a):
+    first = a.astype(BF16)
+    rest = a - first.astype(F32)
+    second = rest.astype(BF16)
+    return first, second, (rest - second.astype(F32)).astype(BF16)
+
+
 def sine_of(angle, shift):
     turns = jnp.floor(angle * (0.5 / math.pi) + (shift + 0.5))
     rest = (angle - turns * TURN_HIGH) - turns * TURN_LOW + shift * (2.0 * math.pi)
@@ -63,6 +70,19 @@
 def forward_kernel(
     rays,
     offsets,
+    frames_far,
+    freq_far,
+    w_in_far,
+    b_in_far,
+    w_mid_far,
+    b_mid_far,
+    w_feat_far,
+    w_dens_far,
+    payload,
+    encoded_far,
+    hidden_one_far,
+    hidden_two_far,
+    kept_far,
     frames,
     freq,
     w_in,
@@ -70,7 +90,7 @@
     w_mid,
     b_mid,
     w_heads,
-    payload,
+    w_dens,
     encoded,
     hidden_one,
     hidden_two,
@@ -79,10 +99,37 @@
     slope,
     heads,
     dens,
+    sent,
+    in_sems,
+    out_sems,
+    last_sems,
 ):
+    wanted = (
+        (frames_far, frames),
+        (freq_far, freq),
+        (w_feat_far, w_heads.at[0:FEAT]),
+        (w_dens_far, w_dens),
+        (w_in_far, w_in),
+        (b_in_far, b_in),
+        (w_mid_far, w_mid),
+        (b_mid_far, b_mid),
+    )
+    arriving = [
+        pltpu.make_async_copy(far, near, in_sems.at[i]) for i, (far, near) in enumerate(wanted)
+    ]
+    for copy in arriving:
+        copy.start()
+    for copy in arriving[:2]:
+        copy.wait()
     lane = lax.broadcasted_iota(jnp.int32, (BLK, 128), 1)
-    columns = jnp.concatenate([frames[...], jnp.zeros((2, RAYS), F32)], axis=0).T
-    both = jnp.concatenate([freq[...], freq[...]], axis=1)
+    columns = jnp.concatenate(
+        [frames[c] for c in range(6)] + [jnp.zeros((2, RAYS), F32)], axis=0
+    ).T
+    both = jnp.concatenate([freq[c] for c in range(3)], axis=0)
+    both = jnp.concatenate([both, both], axis=1)
+    for copy in arriving[2:]:
+        copy.wait()
+    w_heads[FEAT:128, :] = jnp.broadcast_to(w_dens[...].astype(F32), (128 - FEAT, HID)).astype(BF16)
     anchor[...] = (
         columns[:, 0:1] * both[0:1] + columns[:, 1:2] * both[1:2] + columns[:, 2:3] * both[2:3]
     )
@@ -119,6 +166,18 @@
         ]
         return jnp.concatenate(parts, axis=0).astype(BF16)
 
+    def leaving(step):
+        span = pl.ds(pl.multiple_of(step * ROWS, ROWS), ROWS)
+        pairs = (
+            (encoded, encoded_far),
+            (hidden_one, hidden_one_far),
+            (hidden_two, hidden_two_far),
+        )
+        return [
+            pltpu.make_async_copy(near.at[span], far.at[span], out_sems.at[step, i])
+            for i, (near, far) in enumerate(pairs)
+        ]
+
     def chunk(step, carry):
         start = pl.multiple_of(step * ROWS, ROWS)
         enc = jnp.concatenate([encode(step * CHUNK + q) for q in range(CHUNK)], axis=0)
@@ -127,7 +186,7 @@
         hidden_one[pl.ds(start, ROWS), :] = one
         two = jnp.maximum(nn(one, w_mid[...]) + b_mid[...], 0.0).astype(BF16)
         hidden_two[pl.ds(start, ROWS), :] = two
-        both_heads = nn(two, w_heads[...])
+        both_heads = nt(two, w_heads[...])
         heads[pl.ds(start, ROWS), :] = both_heads
         taken = dens[...]
         for q in range(CHUNK):
@@ -135,6 +194,8 @@
                 lane == FEAT + step * CHUNK + q, both_heads[q * BLK : (q + 1) * BLK], taken
             )
         dens[...] = taken
+        for copy in leaving(step):
+            copy.start()
         return carry
 
     lax.fori_loop(0, CAP // CHUNK, chunk, 0)
@@ -153,6 +214,8 @@
     kept[0] = weight
     kept[1] = passed
     kept[2] = jax.nn.sigmoid(pre) * STEP
+    closing = [pltpu.make_async_copy(kept, kept_far, last_sems.at[REGIONS])]
+    closing[0].start()
     last = 1.0 - passed[BLK - 1 : BLK, :]
     lane_row = lane[0:1]
     for slot in range(CAP):
@@ -163,23 +226,39 @@
         )
         row = jnp.where(lane_row < FEAT, colour, last[:, slot : slot + 1])
         row = jnp.where(lane_row == 127, rays[slot].astype(F32), row)
-        payload[slot : slot + 1, :] = row
+        sent[slot : slot + 1, :] = row
+    for peer in range(REGIONS):
+        closing.append(pltpu.make_async_copy(sent, payload.at[peer], last_sems.at[peer]))
+        closing[-1].start()
+    for step in range(CAP // CHUNK):
+        for copy in leaving(step):
+            copy.wait()
+    for copy in closing:
+        copy.wait()
 
 
 def backward_kernel(
-    rays,
     place,
     order,
     gathered,
+    target_far,
+    w_feat_far,
+    w_dens_far,
+    w_mid_far,
+    encoded_far,
+    hidden_one_far,
+    hidden_two_far,
+    kept_far,
+    pixels,
+    packed,
     target,
     w_heads,
+    w_dens,
     w_mid,
     encoded,
     hidden_one,
     hidden_two,
     kept,
-    pixels,
-    packed,
     chosen,
     aim,
     slopes,
@@ -190,7 +269,23 @@
     sum_in,
     bias_mid,
     bias_in,
+    in_sems,
 ):
+    wanted = (
+        (target_far, target),
+        (w_feat_far, w_heads.at[0:FEAT]),
+        (w_dens_far, w_dens),
+        (hidden_two_far, hidden_two),
+        (kept_far, kept),
+        (hidden_one_far, hidden_one),
+        (encoded_far, encoded),
+        (w_mid_far, w_mid),
+    )
+    arriving = [
+        pltpu.make_async_copy(far, near, in_sems.at[i]) for i, (far, near) in enumerate(wanted)
+    ]
+    for copy in arriving:
+        copy.start()
     region = place[0]
     descending = order[0] == 1
     lane = lax.broadcasted_iota(jnp.int32, (BLK, 128), 1)
@@ -216,10 +311,7 @@
             ],
             axis=0,
         )
-        first = rows.astype(BF16)
-        rest = rows - first.astype(F32)
-        second = rest.astype(BF16)
-        third = (rest - second.astype(F32)).astype(BF16)
+        first, second, third = thirds(rows)
         found = (nn(left, third) + nn(left, second)) + nn(left, first)
         chosen[4 * group : 4 * group + 4] = found.reshape(4, 40, 128)
 
@@ -241,27 +333,39 @@
         through = through * through_here
     pixels[...] = total[32:40, :FEAT]
 
-    for slot in range(CAP):
-        slopes[slot : slot + 1, :FEAT] = target[pl.ds(jnp.maximum(rays[slot], 0), 1), :]
+    for copy in arriving[:3]:
+        copy.wait()
+    w_heads[FEAT:128, :] = jnp.broadcast_to(w_dens[...].astype(F32), (128 - FEAT, HID)).astype(BF16)
+    picked = jnp.where(own[:, 127:128] == lane[:CAP].astype(F32), 1.0, 0.0).astype(BF16)
+    first, second, third = thirds(target[...])
+    wished = (nt(picked, third) + nt(picked, second)) + nt(picked, first)
+    wished = jnp.concatenate([wished, jnp.zeros((CAP, 128 - FEAT), F32)], axis=1)
     occupied = (own[:, 127:128] >= 0.0) & (lane[:CAP] < FEAT)
-    scaled = jnp.where(occupied, near[:CAP] * (total[:CAP] - slopes[...]), 0.0)
+    scaled = jnp.where(occupied, near[:CAP] * (total[:CAP] - wished), 0.0)
     inner = jnp.where(occupied, scaled * far[:CAP], 0.0)
     slopes[...] = scaled
     blank = jnp.zeros((96, 128), F32)
     d_through = nt(jnp.ones((8, 128), F32), jnp.concatenate([inner, blank], axis=0), HIGH)[0:1]
     twice = jnp.concatenate([scaled, scaled, blank[:64]], axis=0)
-    direction = nt(w_heads[...].astype(F32), twice, HIGH)
+    direction = lax.dot_general(
+        twice,
+        w_heads[...].astype(F32),
+        (((1,), (0,)), ((), ())),
+        preferred_element_type=F32,
+        precision=HIGH,
+    )
     upper = direction.astype(BF16)
     lower = (direction - upper.astype(F32)).astype(BF16)
     lane_hid = lax.broadcasted_iota(jnp.int32, (HID, 128), 1)
-    aim[...] = jnp.where(lane_hid < CAP, upper.astype(F32), lower.astype(F32)).astype(BF16)
+    slot_row = lax.broadcasted_iota(jnp.int32, (128, HID), 0)
+    aim[...] = jnp.where(slot_row < CAP, upper.astype(F32), lower.astype(F32)).astype(BF16)
 
     proj[...] = jnp.zeros_like(proj)
     slot_lane = jnp.where(lane < 2 * CAP, lane & (CAP - 1), -1)
 
     def project(step, carry):
         start = pl.multiple_of(step * ROWS, ROWS)
-        part = nn(hidden_two[pl.ds(start, ROWS), :], aim[...])
+        part = nt(hidden_two[pl.ds(start, ROWS), :], aim[...])
         taken = proj[...]
         for q in range(CHUNK):
             taken = jnp.where(
@@ -270,6 +374,8 @@
         proj[...] = taken
         return carry
 
+    for copy in arriving[3:]:
+        copy.wait()
     lax.fori_loop(0, CAP // CHUNK, project, 0)
     projected = proj[...] + pltpu.roll(proj[...], 96, 1)
     row_index = lax.broadcasted_iota(jnp.int32, (BLK, BLK), 0)
@@ -303,7 +409,7 @@
         one = hidden_one[pl.ds(start, ROWS), :]
         enc = encoded[pl.ds(start, ROWS), :]
         sum_feat[...] += tn(two, d_heads)
-        d_two = jnp.where(two.astype(F32) > 0.0, nt(d_heads, w_heads[...]), 0.0)
+        d_two = jnp.where(two.astype(F32) > 0.0, nn(d_heads, w_heads[...]), 0.0)
         bias_mid[...] += jnp.sum(d_two.reshape(ROWS // 8, 8, HID), axis=0)
         d_two = d_two.astype(BF16)
         sum_mid[...] += tn(one, d_two)
@@ -346,6 +452,8 @@
 
 VMEM = pl.BlockSpec(memory_space=pltpu.VMEM)
 SMEM = pl.BlockSpec(memory_space=pltpu.SMEM)
+HBM = pl.BlockSpec(memory_space=pltpu.HBM)
+DMA = pltpu.SemaphoreType.DMA
 
 
 def shards(
@@ -365,41 +473,53 @@
     samples = CAP * BLK
     slot_rays = block_rays.reshape(CAP)
     slot_offsets = block_offsets.reshape(CAP)
-    w_heads = jnp.concatenate(
-        [w_feat[0], jnp.broadcast_to(w_dens[0][:, None], (HID, 128 - FEAT))], axis=1
-    )
-    payload, encoded, hidden_one, hidden_two, kept = pl.pallas_call(
+    payload, *stored = pl.pallas_call(
         forward_kernel,
         name="forward",
         out_shape=(
-            jax.ShapeDtypeStruct((CAP, 128), F32),
+            jax.ShapeDtypeStruct((REGIONS, CAP, 128), F32),
             jax.ShapeDtypeStruct((samples, ENC), BF16),
             jax.ShapeDtypeStruct((samples, HID), BF16),
             jax.ShapeDtypeStruct((samples, HID), BF16),
             jax.ShapeDtypeStruct((3, BLK, 128), F32),
         ),
-        in_specs=[SMEM, SMEM] + [VMEM] * 7,
-        out_specs=(VMEM,) * 5,
+        in_specs=[SMEM, SMEM] + [HBM] * 8,
+        out_specs=(HBM,) * 5,
         scratch_shapes=[
+            pltpu.VMEM((6, 1, RAYS), F32),
+            pltpu.VMEM((3, 1, FEAT), F32),
+            pltpu.VMEM((ENC, HID), BF16),
+            pltpu.VMEM((1, HID), F32),
+            pltpu.VMEM((HID, HID), BF16),
+            pltpu.VMEM((1, HID), F32),
+            pltpu.VMEM((128, HID), BF16),
+            pltpu.VMEM((1, HID), BF16),
+            pltpu.VMEM((samples, ENC), BF16),
+            pltpu.VMEM((samples, HID), BF16),
+            pltpu.VMEM((samples, HID), BF16),
+            pltpu.VMEM((3, BLK, 128), F32),
             pltpu.VMEM((RAYS, 128), F32),
             pltpu.VMEM((RAYS, 128), F32),
             pltpu.VMEM((samples, 128), F32),
             pltpu.VMEM((BLK, 128), F32),
+            pltpu.VMEM((CAP, 128), F32),
+            DMA((8,)),
+            DMA((CAP // CHUNK, 3)),
+            DMA((REGIONS + 1,)),
         ],
     )(
         slot_rays,
         slot_offsets,
-        ray_frames[0],
-        enc_freq[0],
+        ray_frames.transpose(1, 0, 2),
+        enc_freq.transpose(1, 0, 2),
         w_in[0],
         b_in,
         w_mid[0],
         b_mid,
-        w_heads,
-    )
-    gathered = lax.all_to_all(
-        jnp.broadcast_to(payload[None], (REGIONS, CAP, 128)), "depth", 0, 0, tiled=True
-    )
+        w_feat[0].T,
+        w_dens,
+    )
+    gathered = lax.all_to_all(payload, "depth", 0, 0, tiled=True)
     place = lax.axis_index("depth").astype(jnp.int32).reshape(1)
     pixels, packed = pl.pallas_call(
         backward_kernel,
@@ -408,11 +528,19 @@
             jax.ShapeDtypeStruct((8, FEAT), F32),
             jax.ShapeDtypeStruct((BATCHES, 32, 128), F32),
         ),
-        in_specs=[SMEM] * 3 + [VMEM] * 8,
+        in_specs=[SMEM] * 2 + [VMEM] + [HBM] * 8,
         out_specs=(VMEM,) * 2,
         scratch_shapes=[
+            pltpu.VMEM((FEAT, RAYS), F32),
+            pltpu.VMEM((128, HID), BF16),
+            pltpu.VMEM((1, HID), BF16),
+            pltpu.VMEM((HID, HID), BF16),
+            pltpu.VMEM((samples, ENC), BF16),
+            pltpu.VMEM((samples, HID), BF16),
+            pltpu.VMEM((samples, HID), BF16),
+            pltpu.VMEM((3, BLK, 128), F32),
             pltpu.VMEM((REGIONS, 40, 128), F32),
-            pltpu.VMEM((HID, 128), BF16),
+            pltpu.VMEM((128, HID), BF16),
             pltpu.VMEM((CAP, 128), F32),
             pltpu.VMEM((BLK, 128), F32),
             pltpu.VMEM((BLK, 128), F32),
@@ -421,19 +549,17 @@
             pltpu.VMEM((ENC, HID), F32),
             pltpu.VMEM((8, HID), F32),
             pltpu.VMEM((8, HID), F32),
+            DMA((8,)),
         ],
     )(
-        slot_rays,
         place,
         view_order,
-        gathered,
-        target[0],
-        w_heads,
+        pltpu.with_memory_space_constraint(gathered, pltpu.VMEM),
+        target[0].T,
+        w_feat[0].T,
+        w_dens,
         w_mid[0],
-        encoded,
-        hidden_one,
-        hidden_two,
-        kept,
+        *stored,
     )
     received = lax.all_to_all(packed, "cam", 0, 0, tiled=True)
     g_in, gb_in, g_mid, gb_mid, g_feat, g_dens = pl.pallas_call(

time: 83.4 us -> 75.2 us (0.902)
  local copies, waits for them, and re-layouts: 7.12 us -> 0 us
  waiting for transfers between devices: 9.62 us -> 11.1 us
  other arithmetic: 1.42 us -> 0 us
  Pallas kernels: 25.5 us -> 24.6 us
    unnamed x6 -> x0, local copies, waits for them, and re-layouts: 5.59 us -> none
    broadcast_in_dim x2 -> x0, local copies, waits for them, and re-layouts: 1.53 us -> none  [the longest x1 1.43 us: shards(): jnp.broadcast_to(payload[None], (REGIONS, CAP, 128))]
    all_to_all x1, waiting for transfers between devices: 9.62 us -> 11.1 us  [shards(): gathered = lax.all_to_all(payload, 'depth', 0, 0, tiled=True)]
  transfers between devices with their start and end apart: 1 -> 1, of which waited for: 1 -> 1; matrix products, arithmetic and copies ran while one was open for 2% -> 0% of each run, Pallas kernels for 0% -> 0%
where the time goes in v2:
time: 75.2 us; the launch traced here: 74.8 us
  blocking collectives  27.7 us (37%)
  Pallas kernels  24.6 us (33%)
  waiting for transfers between devices  11.1 us (15%)
  starting transfers between devices  10.2 us (14%)
  between operations  1.3 us (2%)
    all_to_all x1, blocking collectives, shards(): received = lax.all_to_all(packed, 'cam', 0, 0, tiled=True)  27.7 us
    pallas_call x1, Pallas kernels, shards(): pl.pallas_call(backward_kernel, name='backward', out_shape=(jax.ShapeDtyp...  13.7 us
    all_to_all x1, waiting for transfers between devices, shards(): gathered = lax.all_to_all(payload, 'depth', 0, 0, tiled=True)  11.1 us
    all_to_all x1, starting transfers between devices, shards(): gathered = lax.all_to_all(payload, 'depth', 0, 0, tiled=True)  10.2 us
    pallas_call x1, Pallas kernels, shards(): pl.pallas_call(forward_kernel, name='forward', out_shape=(jax.ShapeDtypeS...  9.06 us
    pallas_call x1, Pallas kernels, shards(): pl.pallas_call(finish_kernel, name='finish', out_shape=(jax.ShapeDtypeStr...  1.78 us
  transfers between devices with their start and end apart: 1, of which 1 were waited for; matrix products, arithmetic and copies ran while one was open for 0% of the time, Pallas kernels for 0%

profile of v2, /device:TPU:1, one launch (start us, length us, event | category | flops | bytes accessed | tf_op | source)
XLA Modules:
  0.0 74.8 jit_solution(17730980550742539738)
XLA Ops:
  0.6 9.1 %forward.1 = (f32[16,32,128]{2,1,0:T(8,128)}, bf16[4096,128]{1,0:T(8,128)(2,1)}, bf16[4096,256]{1,0:T(8,128)(2,1)}, bf16[4096,256]{1,0:T(8,128)(2,1)}, f32[3,128,128]{2,1,0:T(8,128)}) custom-call(s32[32]{0:T(128)} %bitcast.25, s32[32]{0:T(128)} %bitcast.26, f32[6,1,128]{2,1,0:T(1,128)} %bitcast.23, f32[3,1,64]{2,1,0:T(1,128)} %bitcast.24, ...), custom_call_target="tpu_custom_call" | custom-call | tf_op jit(solution)/shard_map/forward/pallas_call | solution.py:476
  9.7 10.2 %all-to-all-start = ((f32[16,32,128]{2,1,0:T(8,128)}), f32[16,32,128]{2,1,0:T(8,128)S(1)}, u32[]{:S(2)}, u32[]{:S(2)}) async-start(f32[16,32,128]{2,1,0:T(8,128)} %get-tuple-element.20), calls=%async_computation | async-start | bytes 524288 | tf_op jit(solution)/shard_map/all_to_all | solution.py:522
  20.5 11.1 %all-to-all-done.gathered = f32[16,32,128]{2,1,0:T(8,128)S(1)} async-done(((f32[16,32,128]{2,1,0:T(8,128)}), f32[16,32,128]{2,1,0:T(8,128)S(1)}, u32[]{:S(2)}, u32[]{:S(2)}) %all-to-all-start) | async-done | bytes 262176 | tf_op jit(solution)/shard_map/all_to_all | solution.py:522
  31.6 13.7 %backward.1 = (f32[8,64]{1,0:T(8,128)}, f32[32,32,128]{2,1,0:T(8,128)}) custom-call(s32[1]{0:T(128)} %bitcast.place, s32[1]{0:T(128)S(6)} %copy.19.order, f32[16,32,128]{2,1,0:T(8,128)S(1)} %all-to-all-done.gathered, f32[64,128]{1,0:T(8,128)} %bitcast.22, bf16[64,256]{1,0:T(8,128)(2,1)} %bitcast.20, bf16[1,256]{1,0:T(2,128)(2,1)} %w_dens_far.3, ...), custom_call_target="tpu_custom_call" | custom-call | tf_op jit(solution)/shard_map/backward/pallas_call | solution.py:524
  45.3 27.7 %all_to_all.10.parts = f32[32,32,128]{2,1,0:T(8,128)} all-to-all(f32[32,32,128]{2,1,0:T(8,128)} %get-tuple-element.26), channel_id=1, replica_groups=mesh['depth'=16,'cam'=32] {'cam'}, dimensions={0} | all-to-all | bytes 1048576 | tf_op jit(solution)/shard_map/all_to_all | solution.py:564
  73.0 1.8 %finish.1 = (f32[4,256]{1,0:T(4,128)}, f32[1,8]{1,0:T(1,128)}, f32[8,256]{1,0:T(8,128)}, f32[1,8]{1,0:T(1,128)}, f32[8,64]{1,0:T(8,128)}, /*index=5*/f32[1,8]{1,0:T(1,128)}) custom-call(f32[32,32,128]{2,1,0:T(8,128)} %all_to_all.10.parts), custom_call_target="tpu_custom_call" | custom-call | tf_op jit(solution)/shard_map/finish/pallas_call | solution.py:565
Async XLA Ops:
  9.7 21.9 %all-to-all-start = ((f32[16,32,128]{2,1,0:T(8,128)}), f32[16,32,128]{2,1,0:T(8,128)S(1)}, u32[]{:S(2)}, u32[]{:S(2)}) async-start(f32[16,32,128]{2,1,0:T(8,128)} %get-tuple-element.20), calls=%async_computation | async-start | bytes 524288 | tf_op jit(solution)/shard_map/all_to_all | solution.py:522

commit v3 on v2

--- a/solution.py
+++ b/solution.py
@@ -16,8 +16,8 @@
 ENC = 128
 REGIONS = 16
 BATCHES = 32
-CHUNK = 4
-ROWS = CHUNK * BLK
+FORWARD_CHUNK = 16
+BACKWARD_CHUNK = 8
 STEP = 1.0 / 64.0
 F32 = jnp.float32
 BF16 = jnp.bfloat16
@@ -55,6 +55,18 @@
     rest = a - first.astype(F32)
     second = rest.astype(BF16)
     return first, second, (rest - second.astype(F32)).astype(BF16)
+
+
+def stacked(a, parts):
+    return jnp.concatenate(thirds(a)[:parts], axis=0)
+
+
+def folded(a, parts):
+    rows = a.shape[0] // parts
+    total = a[(parts - 1) * rows :]
+    for part in range(parts - 2, -1, -1):
+        total = total + a[part * rows : (part + 1) * rows]
+    return total
 
 
 def sine_of(angle, shift):
@@ -97,7 +109,6 @@
     kept,
     anchor,
     slope,
-    heads,
     dens,
     sent,
     in_sems,
@@ -121,6 +132,7 @@
         copy.start()
     for copy in arriving[:2]:
         copy.wait()
+    rows_each = FORWARD_CHUNK * BLK
     lane = lax.broadcasted_iota(jnp.int32, (BLK, 128), 1)
     columns = jnp.concatenate(
         [frames[c] for c in range(6)] + [jnp.zeros((2, RAYS), F32)], axis=0
@@ -167,7 +179,7 @@
         return jnp.concatenate(parts, axis=0).astype(BF16)
 
     def leaving(step):
-        span = pl.ds(pl.multiple_of(step * ROWS, ROWS), ROWS)
+        span = pl.ds(pl.multiple_of(step * rows_each, rows_each), rows_each)
         pairs = (
             (encoded, encoded_far),
             (hidden_one, hidden_one_far),
@@ -179,34 +191,31 @@
         ]
 
     def chunk(step, carry):
-        start = pl.multiple_of(step * ROWS, ROWS)
-        enc = jnp.concatenate([encode(step * CHUNK + q) for q in range(CHUNK)], axis=0)
-        encoded[pl.ds(start, ROWS), :] = enc
+        start = pl.multiple_of(step * rows_each, rows_each)
+        enc = jnp.concatenate([encode(step * FORWARD_CHUNK + q) for q in range(FORWARD_CHUNK)], axis=0)
+        encoded[pl.ds(start, rows_each), :] = enc
         one = jnp.maximum(nn(enc, w_in[...]) + b_in[...], 0.0).astype(BF16)
-        hidden_one[pl.ds(start, ROWS), :] = one
+        hidden_one[pl.ds(start, rows_each), :] = one
         two = jnp.maximum(nn(one, w_mid[...]) + b_mid[...], 0.0).astype(BF16)
-        hidden_two[pl.ds(start, ROWS), :] = two
+        hidden_two[pl.ds(start, rows_each), :] = two
         both_heads = nt(two, w_heads[...])
-        heads[pl.ds(start, ROWS), :] = both_heads
         taken = dens[...]
-        for q in range(CHUNK):
+        for q in range(FORWARD_CHUNK):
             taken = jnp.where(
-                lane == FEAT + step * CHUNK + q, both_heads[q * BLK : (q + 1) * BLK], taken
+                lane == FEAT + step * FORWARD_CHUNK + q, both_heads[q * BLK : (q + 1) * BLK], taken
             )
         dens[...] = taken
         for copy in leaving(step):
             copy.start()
         return carry
 
-    lax.fori_loop(0, CAP // CHUNK, chunk, 0)
-
-    pre = pltpu.roll(dens[...], 64, 1)
+    lax.fori_loop(0, CAP // FORWARD_CHUNK, chunk, 0)
+
+    pre = dens[...].T[FEAT : FEAT + CAP]
     tau = (jnp.maximum(pre, 0.0) + jnp.log1p(jnp.exp(-jnp.abs(pre)))) * STEP
     row_index = lax.broadcasted_iota(jnp.int32, (BLK, BLK), 0)
-    earlier = (lane < row_index).astype(F32)
-    before = lax.dot_general(
-        earlier, tau, (((1,), (0,)), ((), ())), preferred_element_type=F32, precision=HIGH
-    )
+    earlier = jnp.where(row_index < lane, 1.0, 0.0).astype(BF16)
+    before = folded(nn(stacked(tau, 3), earlier), 3)
     series = tau * (1.0 - tau * (0.5 - tau * (1.0 / 6.0 - tau * (1.0 / 24.0))))
     opacity = jnp.where(tau < 0.03, series, 1.0 - jnp.exp(-tau))
     weight = jnp.exp(-before) * opacity
@@ -216,21 +225,29 @@
     kept[2] = jax.nn.sigmoid(pre) * STEP
     closing = [pltpu.make_async_copy(kept, kept_far, last_sems.at[REGIONS])]
     closing[0].start()
-    last = 1.0 - passed[BLK - 1 : BLK, :]
-    lane_row = lane[0:1]
-    for slot in range(CAP):
-        colour = jnp.sum(
-            weight[:, slot : slot + 1] * heads[slot * BLK : (slot + 1) * BLK, :],
-            axis=0,
-            keepdims=True,
-        )
-        row = jnp.where(lane_row < FEAT, colour, last[:, slot : slot + 1])
-        row = jnp.where(lane_row == 127, rays[slot].astype(F32), row)
-        sent[slot : slot + 1, :] = row
+    weight_parts = stacked(weight, 2).astype(F32)
+    slot_row = lax.broadcasted_iota(jnp.int32, (2 * CAP, 128), 0) & (CAP - 1)
+    spread = jnp.concatenate(
+        [jnp.where(slot_row == slot, weight_parts, 0.0).astype(BF16) for slot in range(CAP)],
+        axis=1,
+    )
+    blended = folded(nn(spread, hidden_two[...]), 2)
+    colour = folded(nt(stacked(blended, 2), w_heads[...]), 2)
+    row8 = lax.broadcasted_iota(jnp.int32, (8, 128), 0)
+    names = []
+    for tile in range(CAP // 8):
+        name = jnp.zeros((8, 128), F32)
+        for k in range(8):
+            name = jnp.where(row8 == k, rays[8 * tile + k].astype(F32), name)
+        names.append(name)
+    names = jnp.concatenate(names, axis=0)
+    lane_row = lane[:CAP]
+    row = jnp.where(lane_row < FEAT, colour, 1.0 - passed[:, BLK - 1 : BLK])
+    sent[...] = jnp.where(lane_row == 127, names, row)
     for peer in range(REGIONS):
         closing.append(pltpu.make_async_copy(sent, payload.at[peer], last_sems.at[peer]))
         closing[-1].start()
-    for step in range(CAP // CHUNK):
+    for step in range(CAP // FORWARD_CHUNK):
         for copy in leaving(step):
             copy.wait()
     for copy in closing:
@@ -263,7 +280,7 @@
     aim,
     slopes,
     proj,
-    pre_grad,
+    columns,
     sum_feat,
     sum_mid,
     sum_in,
@@ -286,6 +303,7 @@
     ]
     for copy in arriving:
         copy.start()
+    rows_each = BACKWARD_CHUNK * BLK
     region = place[0]
     descending = order[0] == 1
     lane = lax.broadcasted_iota(jnp.int32, (BLK, 128), 1)
@@ -298,20 +316,17 @@
         ],
         axis=0,
     )
-    picker = (lax.broadcasted_iota(jnp.int32, (8, 128), 1) == 127).astype(F32)
+    picker = jnp.where(lane[:16] == 127, 1.0, 0.0).astype(BF16)
     group_of = lax.broadcasted_iota(jnp.int32, (40, 128), 1) // CAP
     for group in range(4):
         rows = gathered[4 * group : 4 * group + 4].reshape(128, 128)
-        names = nt(picker, rows, HIGH)[0:1]
+        first, second, third = thirds(rows)
+        names = nt(picker, first)[0:1]
         same = wanted == names
         left = jnp.concatenate(
-            [
-                jnp.where(same & (group_of == k), 1.0, 0.0).astype(BF16)
-                for k in range(4)
-            ],
+            [jnp.where(same & (group_of == k), 1.0, 0.0).astype(BF16) for k in range(4)],
             axis=0,
         )
-        first, second, third = thirds(rows)
         found = (nn(left, third) + nn(left, second)) + nn(left, first)
         chosen[4 * group : 4 * group + 4] = found.reshape(4, 40, 128)
 
@@ -344,81 +359,71 @@
     scaled = jnp.where(occupied, near[:CAP] * (total[:CAP] - wished), 0.0)
     inner = jnp.where(occupied, scaled * far[:CAP], 0.0)
     slopes[...] = scaled
-    blank = jnp.zeros((96, 128), F32)
-    d_through = nt(jnp.ones((8, 128), F32), jnp.concatenate([inner, blank], axis=0), HIGH)[0:1]
-    twice = jnp.concatenate([scaled, scaled, blank[:64]], axis=0)
-    direction = lax.dot_general(
-        twice,
-        w_heads[...].astype(F32),
-        (((1,), (0,)), ((), ())),
-        preferred_element_type=F32,
-        precision=HIGH,
-    )
+    d_through = jnp.sum(inner, axis=1, keepdims=True)
+    direction = folded(nn(stacked(scaled, 3), w_heads[...]), 3)
     upper = direction.astype(BF16)
     lower = (direction - upper.astype(F32)).astype(BF16)
-    lane_hid = lax.broadcasted_iota(jnp.int32, (HID, 128), 1)
-    slot_row = lax.broadcasted_iota(jnp.int32, (128, HID), 0)
-    aim[...] = jnp.where(slot_row < CAP, upper.astype(F32), lower.astype(F32)).astype(BF16)
+    aim[0:CAP, :] = upper
+    aim[CAP : 2 * CAP, :] = lower
+    aim[2 * CAP : 128, :] = jnp.zeros((128 - 2 * CAP, HID), BF16)
 
     proj[...] = jnp.zeros_like(proj)
     slot_lane = jnp.where(lane < 2 * CAP, lane & (CAP - 1), -1)
 
     def project(step, carry):
-        start = pl.multiple_of(step * ROWS, ROWS)
-        part = nt(hidden_two[pl.ds(start, ROWS), :], aim[...])
+        start = pl.multiple_of(step * rows_each, rows_each)
+        part = nt(hidden_two[pl.ds(start, rows_each), :], aim[...])
         taken = proj[...]
-        for q in range(CHUNK):
+        for q in range(BACKWARD_CHUNK):
             taken = jnp.where(
-                slot_lane == step * CHUNK + q, part[q * BLK : (q + 1) * BLK], taken
+                slot_lane == step * BACKWARD_CHUNK + q, part[q * BLK : (q + 1) * BLK], taken
             )
         proj[...] = taken
         return carry
 
-    for copy in arriving[3:]:
+    arriving[3].wait()
+    lax.fori_loop(0, CAP // BACKWARD_CHUNK, project, 0)
+    turned = proj[...].T
+    projected = turned[0:CAP] + turned[CAP : 2 * CAP]
+    arriving[4].wait()
+    row_index = lax.broadcasted_iota(jnp.int32, (BLK, BLK), 0)
+    later = jnp.where(row_index > lane, 1.0, 0.0).astype(BF16)
+    weight, passed = kept[0], kept[1]
+    behind = folded(nn(stacked(projected * weight, 3), later), 3)
+    d_tau = projected * passed - behind - d_through * passed[:, BLK - 1 : BLK]
+    columns[...] = jnp.concatenate(
+        [weight, d_tau * kept[2], jnp.zeros((128 - 2 * CAP, BLK), F32)], axis=0
+    ).T
+    for copy in arriving[5:]:
         copy.wait()
-    lax.fori_loop(0, CAP // CHUNK, project, 0)
-    projected = proj[...] + pltpu.roll(proj[...], 96, 1)
-    row_index = lax.broadcasted_iota(jnp.int32, (BLK, BLK), 0)
-    later = (lane > row_index).astype(F32)
-    weight, passed = kept[0], kept[1]
-    behind = lax.dot_general(
-        later,
-        projected * weight,
-        (((1,), (0,)), ((), ())),
-        preferred_element_type=F32,
-        precision=HIGH,
-    )
-    d_tau = projected * passed - behind - d_through * passed[BLK - 1 : BLK, :]
-    pre_grad[...] = d_tau * kept[2]
 
     for ref in (sum_feat, sum_mid, sum_in, bias_mid, bias_in):
         ref[...] = jnp.zeros_like(ref)
 
     def chunk(step, carry):
-        start = pl.multiple_of(step * ROWS, ROWS)
-        turn = lax.rem(128 - step * CHUNK, 128)
-        weights = pltpu.roll(kept[0], turn, 1)
-        pres = pltpu.roll(pre_grad[...], turn, 1)
+        start = pl.multiple_of(step * rows_each, rows_each)
+        turn = lax.rem(128 - step * BACKWARD_CHUNK, 128)
+        here = pltpu.roll(columns[...], turn, 1)
         parts = []
-        for q in range(CHUNK):
-            colour = slopes[pl.ds(step * CHUNK + q, 1), :]
-            pre_here = jnp.where(lane == FEAT, pres[:, q : q + 1], 0.0)
-            parts.append(jnp.where(lane < FEAT, weights[:, q : q + 1] * colour, pre_here))
+        for q in range(BACKWARD_CHUNK):
+            colour = slopes[pl.ds(step * BACKWARD_CHUNK + q, 1), :]
+            pre_here = jnp.where(lane == FEAT, here[:, CAP + q : CAP + q + 1], 0.0)
+            parts.append(jnp.where(lane < FEAT, here[:, q : q + 1] * colour, pre_here))
         d_heads = jnp.concatenate(parts, axis=0).astype(BF16)
-        two = hidden_two[pl.ds(start, ROWS), :]
-        one = hidden_one[pl.ds(start, ROWS), :]
-        enc = encoded[pl.ds(start, ROWS), :]
+        two = hidden_two[pl.ds(start, rows_each), :]
+        one = hidden_one[pl.ds(start, rows_each), :]
+        enc = encoded[pl.ds(start, rows_each), :]
         sum_feat[...] += tn(two, d_heads)
         d_two = jnp.where(two.astype(F32) > 0.0, nn(d_heads, w_heads[...]), 0.0)
-        bias_mid[...] += jnp.sum(d_two.reshape(ROWS // 8, 8, HID), axis=0)
+        bias_mid[...] += jnp.sum(d_two.reshape(rows_each // 8, 8, HID), axis=0)
         d_two = d_two.astype(BF16)
         sum_mid[...] += tn(one, d_two)
         d_one = jnp.where(one.astype(F32) > 0.0, nt(d_two, w_mid[...]), 0.0)
-        bias_in[...] += jnp.sum(d_one.reshape(ROWS // 8, 8, HID), axis=0)
+        bias_in[...] += jnp.sum(d_one.reshape(rows_each // 8, 8, HID), axis=0)
         sum_in[...] += tn(enc, d_one.astype(BF16))
         return carry
 
-    lax.fori_loop(0, CAP // CHUNK, chunk, 0)
+    lax.fori_loop(0, CAP // BACKWARD_CHUNK, chunk, 0)
 
     spread = jnp.concatenate(
         [
@@ -428,7 +433,7 @@
         ],
         axis=0,
     ).T
-    sum_feat[...] = jnp.where(lane_hid < 96, sum_feat[...], spread)
+    sum_feat[...] = jnp.where(lax.broadcasted_iota(jnp.int32, (HID, 128), 1) < 96, sum_feat[...], spread)
     for part in range(BATCHES):
         packed[part, 0:8, :] = sum_mid[8 * part : 8 * part + 8, 0:128]
         packed[part, 8:16, :] = sum_mid[8 * part : 8 * part + 8, 128:256]
@@ -481,7 +486,7 @@
             jax.ShapeDtypeStruct((samples, ENC), BF16),
             jax.ShapeDtypeStruct((samples, HID), BF16),
             jax.ShapeDtypeStruct((samples, HID), BF16),
-            jax.ShapeDtypeStruct((3, BLK, 128), F32),
+            jax.ShapeDtypeStruct((3, CAP, BLK), F32),
         ),
         in_specs=[SMEM, SMEM] + [HBM] * 8,
         out_specs=(HBM,) * 5,
@@ -497,14 +502,13 @@
             pltpu.VMEM((samples, ENC), BF16),
             pltpu.VMEM((samples, HID), BF16),
             pltpu.VMEM((samples, HID), BF16),
-            pltpu.VMEM((3, BLK, 128), F32),
+            pltpu.VMEM((3, CAP, BLK), F32),
             pltpu.VMEM((RAYS, 128), F32),
             pltpu.VMEM((RAYS, 128), F32),
-            pltpu.VMEM((samples, 128), F32),
             pltpu.VMEM((BLK, 128), F32),
             pltpu.VMEM((CAP, 128), F32),
             DMA((8,)),
-            DMA((CAP // CHUNK, 3)),
+            DMA((CAP // FORWARD_CHUNK, 3)),
             DMA((REGIONS + 1,)),
         ],
     )(
@@ -538,7 +542,7 @@
             pltpu.VMEM((samples, ENC), BF16),
             pltpu.VMEM((samples, HID), BF16),
             pltpu.VMEM((samples, HID), BF16),
-            pltpu.VMEM((3, BLK, 128), F32),
+            pltpu.VMEM((3, CAP, BLK), F32),
             pltpu.VMEM((REGIONS, 40, 128), F32),
             pltpu.VMEM((128, HID), BF16),
             pltpu.VMEM((CAP, 128), F32),
@@ -575,7 +579,7 @@
         ),
         in_specs=[VMEM],
         out_specs=(VMEM,) * 6,
-    )(received)
+    )(pltpu.with_memory_space_constraint(received, pltpu.VMEM))
     return (pixels[None], g_in[None], gb_in, g_mid[None], gb_mid, g_feat[None], g_dens)
 
 

time: 75.2 us -> 67.4 us (0.90)
  Pallas kernels: 24.6 us -> 16.8 us
    pallas_call x1, Pallas kernels: 13.7 us -> 9.73 us  [shards(): pl.pallas_call(backward_kernel, name='backward', out_shape=(jax.ShapeDtyp...]
    pallas_call x1, Pallas kernels: 9.06 us -> 6.31 us  [shards(): pl.pallas_call(forward_kernel, name='forward', out_shape=(jax.ShapeDtypeS...]
    pallas_call x1, Pallas kernels: 1.78 us -> 0.73 us  [shards(): pl.pallas_call(finish_kernel, name='finish', out_shape=(jax.ShapeDtypeStr...]
where the time goes in v3:
time: 67.4 us; the launch traced here: 66.9 us
  blocking collectives  27.6 us (41%)
  Pallas kernels  16.8 us (25%)
  waiting for transfers between devices  11.1 us (16%)
  starting transfers between devices  10.2 us (15%)
  between operations  1.3 us (2%)
    all_to_all x1, blocking collectives, shards(): received = lax.all_to_all(packed, 'cam', 0, 0, tiled=True)  27.6 us
    all_to_all x1, waiting for transfers between devices, shards(): gathered = lax.all_to_all(payload, 'depth', 0, 0, tiled=True)  11.1 us
    all_to_all x1, starting transfers between devices, shards(): gathered = lax.all_to_all(payload, 'depth', 0, 0, tiled=True)  10.2 us
    pallas_call x1, Pallas kernels, shards(): pl.pallas_call(backward_kernel, name='backward', out_shape=(jax.ShapeDtyp...  9.73 us
    pallas_call x1, Pallas kernels, shards(): pl.pallas_call(forward_kernel, name='forward', out_shape=(jax.ShapeDtypeS...  6.31 us
  transfers between devices with their start and end apart: 1, of which 1 were waited for; matrix products, arithmetic and copies ran while one was open for 0% of the time, Pallas kernels for 0%

profile of v3, /device:TPU:1, one launch (start us, length us, event | category | flops | bytes accessed | tf_op | source)
XLA Modules:
  0.0 66.9 jit_solution(15899162965045604178)
XLA Ops:
  0.6 6.3 %forward.1 = (f32[16,32,128]{2,1,0:T(8,128)}, bf16[4096,128]{1,0:T(8,128)(2,1)}, bf16[4096,256]{1,0:T(8,128)(2,1)}, bf16[4096,256]{1,0:T(8,128)(2,1)}, f32[3,32,128]{2,1,0:T(8,128)}) custom-call(s32[32]{0:T(128)} %bitcast.25, s32[32]{0:T(128)} %bitcast.26, f32[6,1,128]{2,1,0:T(1,128)} %bitcast.23, f32[3,1,64]{2,1,0:T(1,128)} %bitcast.24, ...), custom_call_target="tpu_custom_call" | custom-call | tf_op jit(solution)/shard_map/forward/pallas_call | solution.py:481
  7.0 10.2 %all-to-all-start = ((f32[16,32,128]{2,1,0:T(8,128)}), f32[16,32,128]{2,1,0:T(8,128)S(1)}, u32[]{:S(2)}, u32[]{:S(2)}) async-start(f32[16,32,128]{2,1,0:T(8,128)} %get-tuple-element.20), calls=%async_computation | async-start | bytes 524288 | tf_op jit(solution)/shard_map/all_to_all | solution.py:526
  17.8 11.1 %all-to-all-done.gathered = f32[16,32,128]{2,1,0:T(8,128)S(1)} async-done(((f32[16,32,128]{2,1,0:T(8,128)}), f32[16,32,128]{2,1,0:T(8,128)S(1)}, u32[]{:S(2)}, u32[]{:S(2)}) %all-to-all-start) | async-done | bytes 262176 | tf_op jit(solution)/shard_map/all_to_all | solution.py:526
  28.9 9.7 %backward.1 = (f32[8,64]{1,0:T(8,128)}, f32[32,32,128]{2,1,0:T(8,128)}) custom-call(s32[1]{0:T(128)} %bitcast.place, s32[1]{0:T(128)S(6)} %copy.19.order, f32[16,32,128]{2,1,0:T(8,128)S(1)} %all-to-all-done.gathered, f32[64,128]{1,0:T(8,128)} %bitcast.22, bf16[64,256]{1,0:T(8,128)(2,1)} %bitcast.20, bf16[1,256]{1,0:T(2,128)(2,1)} %w_dens_far.3, ...), custom_call_target="tpu_custom_call" | custom-call | tf_op jit(solution)/shard_map/backward/pallas_call | solution.py:528
  38.6 27.6 %all_to_all.10.parts = f32[32,32,128]{2,1,0:T(8,128)S(1)} all-to-all(f32[32,32,128]{2,1,0:T(8,128)} %get-tuple-element.26), channel_id=1, replica_groups=mesh['depth'=16,'cam'=32] {'cam'}, dimensions={0} | all-to-all | bytes 1048576 | tf_op jit(solution)/shard_map/all_to_all | solution.py:568
  66.2 0.7 %finish.1 = (f32[4,256]{1,0:T(4,128)}, f32[1,8]{1,0:T(1,128)}, f32[8,256]{1,0:T(8,128)}, f32[1,8]{1,0:T(1,128)}, f32[8,64]{1,0:T(8,128)}, /*index=5*/f32[1,8]{1,0:T(1,128)}) custom-call(f32[32,32,128]{2,1,0:T(8,128)S(1)} %all_to_all.10.parts), custom_call_target="tpu_custom_call" | custom-call | tf_op jit(solution)/shard_map/finish/pallas_call | solution.py:569
Async XLA Ops:
  7.0 21.9 %all-to-all-start = ((f32[16,32,128]{2,1,0:T(8,128)}), f32[16,32,128]{2,1,0:T(8,128)S(1)}, u32[]{:S(2)}, u32[]{:S(2)}) async-start(f32[16,32,128]{2,1,0:T(8,128)} %get-tuple-element.20), calls=%async_computation | async-start | bytes 524288 | tf_op jit(solution)/shard_map/all_to_all | solution.py:526

commit v4 on v3

--- a/solution.py
+++ b/solution.py
@@ -18,6 +18,7 @@
 BATCHES = 32
 FORWARD_CHUNK = 16
 BACKWARD_CHUNK = 8
+LINES = CAP * FEAT // 128 + 1
 STEP = 1.0 / 64.0
 F32 = jnp.float32
 BF16 = jnp.bfloat16
@@ -241,11 +242,20 @@
             name = jnp.where(row8 == k, rays[8 * tile + k].astype(F32), name)
         names.append(name)
     names = jnp.concatenate(names, axis=0)
-    lane_row = lane[:CAP]
-    row = jnp.where(lane_row < FEAT, colour, 1.0 - passed[:, BLK - 1 : BLK])
-    sent[...] = jnp.where(lane_row == 127, names, row)
+    blocked = jnp.broadcast_to(1.0 - passed[:, BLK - 1 : BLK], (CAP, 128))
+    closing_row = jnp.concatenate(
+        [blocked, names, jnp.zeros((128 - 2 * CAP, 128), F32)], axis=0
+    ).T[0:1]
+    pairs = jnp.where(lane[:16] < FEAT, colour[:16], pltpu.roll(colour[16:], FEAT, 1))
+    for i in range(16):
+        sent[i] = pairs[i : i + 1]
+    sent[16] = closing_row
     for peer in range(REGIONS):
-        closing.append(pltpu.make_async_copy(sent, payload.at[peer], last_sems.at[peer]))
+        closing.append(
+            pltpu.make_async_copy(
+                sent, payload.at[pl.ds(LINES * peer, LINES)], last_sems.at[peer]
+            )
+        )
         closing[-1].start()
     for step in range(CAP // FORWARD_CHUNK):
         for copy in leaving(step):
@@ -308,20 +318,33 @@
     descending = order[0] == 1
     lane = lax.broadcasted_iota(jnp.int32, (BLK, 128), 1)
 
-    own = gathered[region]
+    closing_rows = jnp.concatenate(
+        [gathered[LINES * j + LINES - 1] for j in range(REGIONS)], axis=0
+    )
+    closing_columns = jnp.concatenate(
+        [closing_rows, jnp.zeros((128 - REGIONS, 128), F32)], axis=0
+    ).T
+    own = jnp.sum(
+        jnp.where(lane[:CAP] == region, closing_columns[CAP : 2 * CAP], 0.0),
+        axis=1,
+        keepdims=True,
+    )
     wanted = jnp.concatenate(
-        [
-            own[:, 127:128],
-            (lax.broadcasted_iota(jnp.int32, (8, 1), 0) + 8 * region).astype(F32),
-        ],
+        [own, (lax.broadcasted_iota(jnp.int32, (8, 1), 0) + 8 * region).astype(F32)],
         axis=0,
     )
-    picker = jnp.where(lane[:16] == 127, 1.0, 0.0).astype(BF16)
     group_of = lax.broadcasted_iota(jnp.int32, (40, 128), 1) // CAP
     for group in range(4):
-        rows = gathered[4 * group : 4 * group + 4].reshape(128, 128)
-        first, second, third = thirds(rows)
-        names = nt(picker, first)[0:1]
+        tiles = []
+        names = jnp.zeros((1, 128), F32)
+        for k in range(4):
+            j = 4 * group + k
+            pairs = gathered[LINES * j : LINES * j + 16].reshape(16, 128)
+            colours = jnp.concatenate([pairs, pltpu.roll(pairs, FEAT, 1)], axis=0)
+            tiles.append(jnp.where(lane[:CAP] < FEAT, colours, closing_columns[:CAP, j : j + 1]))
+            turned = pltpu.roll(closing_rows[j : j + 1], (CAP * (k - 1)) % 128, 1)
+            names = jnp.where(group_of[0:1] == k, turned, names)
+        first, second, third = thirds(jnp.concatenate(tiles, axis=0))
         same = wanted == names
         left = jnp.concatenate(
             [jnp.where(same & (group_of == k), 1.0, 0.0).astype(BF16) for k in range(4)],
@@ -351,11 +374,11 @@
     for copy in arriving[:3]:
         copy.wait()
     w_heads[FEAT:128, :] = jnp.broadcast_to(w_dens[...].astype(F32), (128 - FEAT, HID)).astype(BF16)
-    picked = jnp.where(own[:, 127:128] == lane[:CAP].astype(F32), 1.0, 0.0).astype(BF16)
+    picked = jnp.where(own == lane[:CAP].astype(F32), 1.0, 0.0).astype(BF16)
     first, second, third = thirds(target[...])
     wished = (nt(picked, third) + nt(picked, second)) + nt(picked, first)
     wished = jnp.concatenate([wished, jnp.zeros((CAP, 128 - FEAT), F32)], axis=1)
-    occupied = (own[:, 127:128] >= 0.0) & (lane[:CAP] < FEAT)
+    occupied = (own >= 0.0) & (lane[:CAP] < FEAT)
     scaled = jnp.where(occupied, near[:CAP] * (total[:CAP] - wished), 0.0)
     inner = jnp.where(occupied, scaled * far[:CAP], 0.0)
     slopes[...] = scaled
@@ -482,7 +505,7 @@
         forward_kernel,
         name="forward",
         out_shape=(
-            jax.ShapeDtypeStruct((REGIONS, CAP, 128), F32),
+            jax.ShapeDtypeStruct((REGIONS * LINES, 1, 128), F32),
             jax.ShapeDtypeStruct((samples, ENC), BF16),
             jax.ShapeDtypeStruct((samples, HID), BF16),
             jax.ShapeDtypeStruct((samples, HID), BF16),
@@ -506,7 +529,7 @@
             pltpu.VMEM((RAYS, 128), F32),
             pltpu.VMEM((RAYS, 128), F32),
             pltpu.VMEM((BLK, 128), F32),
-            pltpu.VMEM((CAP, 128), F32),
+            pltpu.VMEM((LINES, 1, 128), F32),
             DMA((8,)),
             DMA((CAP // FORWARD_CHUNK, 3)),
             DMA((REGIONS + 1,)),

time: 67.4 us -> 65.1 us (0.966)
  the two profiles are of different devices: /device:TPU:1 before, /device:TPU:64 now
where the time goes in v4:
time: 65.1 us; the launch traced here: 64.7 us
  blocking collectives  31.1 us (48%)
  Pallas kernels  16.9 us (26%)
  waiting for transfers between devices  8.15 us (13%)
  starting transfers between devices  7.22 us (11%)
  between operations  1.31 us (2%)
    all_to_all x1, blocking collectives, shards(): received = lax.all_to_all(packed, 'cam', 0, 0, tiled=True)  31.1 us
    pallas_call x1, Pallas kernels, shards(): pl.pallas_call(backward_kernel, name='backward', out_shape=(jax.ShapeDtyp...  9.81 us
    all_to_all x1, waiting for transfers between devices, shards(): gathered = lax.all_to_all(payload, 'depth', 0, 0, tiled=True)  8.15 us
    all_to_all x1, starting transfers between devices, shards(): gathered = lax.all_to_all(payload, 'depth', 0, 0, tiled=True)  7.22 us
    pallas_call x1, Pallas kernels, shards(): pl.pallas_call(forward_kernel, name='forward', out_shape=(jax.ShapeDtypeS...  6.37 us
  transfers between devices with their start and end apart: 1, of which 1 were waited for; matrix products, arithmetic and copies ran while one was open for 0% of the time, Pallas kernels for 0%

profile of v4, /device:TPU:64, one launch (start us, length us, event | category | flops | bytes accessed | tf_op | source)
XLA Modules:
  0.0 64.7 jit_solution(11689073286300172371)
XLA Ops:
  0.6 6.4 %forward.1 = (f32[272,1,128]{2,1,0:T(1,128)}, bf16[4096,128]{1,0:T(8,128)(2,1)}, bf16[4096,256]{1,0:T(8,128)(2,1)}, bf16[4096,256]{1,0:T(8,128)(2,1)}, f32[3,32,128]{2,1,0:T(8,128)}) custom-call(s32[32]{0:T(128)} %bitcast.25, s32[32]{0:T(128)} %bitcast.26, f32[6,1,128]{2,1,0:T(1,128)} %bitcast.23, f32[3,1,64]{2,1,0:T(1,128)} %bitcast.24, ...), custom_call_target="tpu_custom_call" | custom-call | tf_op jit(solution)/shard_map/forward/pallas_call | solution.py:504
  7.0 7.2 %all-to-all-start = ((f32[272,1,128]{2,1,0:T(1,128)}), f32[272,1,128]{2,1,0:T(1,128)S(1)}, u32[]{:S(2)}, u32[]{:S(2)}) async-start(f32[272,1,128]{2,1,0:T(1,128)} %get-tuple-element.20), calls=%async_computation | async-start | bytes 278528 | tf_op jit(solution)/shard_map/all_to_all | solution.py:549
  14.9 8.2 %all-to-all-done.gathered = f32[272,1,128]{2,1,0:T(1,128)S(1)} async-done(((f32[272,1,128]{2,1,0:T(1,128)}), f32[272,1,128]{2,1,0:T(1,128)S(1)}, u32[]{:S(2)}, u32[]{:S(2)}) %all-to-all-start) | async-done | bytes 139296 | tf_op jit(solution)/shard_map/all_to_all | solution.py:549
  23.0 9.8 %backward.1 = (f32[8,64]{1,0:T(8,128)}, f32[32,32,128]{2,1,0:T(8,128)}) custom-call(s32[1]{0:T(128)} %bitcast.place, s32[1]{0:T(128)S(6)} %copy.19.order, f32[272,1,128]{2,1,0:T(1,128)S(1)} %all-to-all-done.gathered, f32[64,128]{1,0:T(8,128)} %bitcast.22, bf16[64,256]{1,0:T(8,128)(2,1)} %bitcast.20, bf16[1,256]{1,0:T(2,128)(2,1)} %w_dens_far.3, ...), custom_call_target="tpu_custom_call" | custom-call | tf_op jit(solution)/shard_map/backward/pallas_call | solution.py:551
  32.9 31.1 %all_to_all.10.parts = f32[32,32,128]{2,1,0:T(8,128)S(1)} all-to-all(f32[32,32,128]{2,1,0:T(8,128)} %get-tuple-element.26), channel_id=1, replica_groups=mesh['depth'=16,'cam'=32] {'cam'}, dimensions={0} | all-to-all | bytes 1048576 | tf_op jit(solution)/shard_map/all_to_all | solution.py:591
  63.9 0.7 %finish.1 = (f32[4,256]{1,0:T(4,128)}, f32[1,8]{1,0:T(1,128)}, f32[8,256]{1,0:T(8,128)}, f32[1,8]{1,0:T(1,128)}, f32[8,64]{1,0:T(8,128)}, /*index=5*/f32[1,8]{1,0:T(1,128)}) custom-call(f32[32,32,128]{2,1,0:T(8,128)S(1)} %all_to_all.10.parts), custom_call_target="tpu_custom_call" | custom-call | tf_op jit(solution)/shard_map/finish/pallas_call | solution.py:592
Async XLA Ops:
  7.0 16.0 %all-to-all-start = ((f32[272,1,128]{2,1,0:T(1,128)}), f32[272,1,128]{2,1,0:T(1,128)S(1)}, u32[]{:S(2)}, u32[]{:S(2)}) async-start(f32[272,1,128]{2,1,0:T(1,128)} %get-tuple-element.20), calls=%async_computation | async-start | bytes 278528 | tf_op jit(solution)/shard_map/all_to_all | solution.py:549
